TPU v7x, 128 devices: a whole 4x4x4 slice. The times are simulated.
128 devices in a mesh: tm: 4 (over z), ent: 32 (over x, y, core).
Axes of the slice: x: 4, y: 4, z: 4, core: 2. Of those that a mesh axis runs over, the one named last changes fastest.
Arguments:
- states: bfloat16 [4, 32768, 512], P('tm', 'ent'), may hold values from -6 to 6
- cotangent: bfloat16 [4, 32768, 512], P('tm', 'ent'), may hold values from -6 to 6
- export_rows: int32 [4, 32768], P('tm', 'ent'), may hold values from 0 to 1023
- edge_src: int32 [4, 32768], P('tm', 'ent'), may hold values from 0 to 1023
- edge_dst: int32 [4, 32768], P('tm', 'ent'), may hold values from 0 to 1023
- edge_rel: int32 [4, 32768], P('tm', 'ent'), may hold values from 0 to 255
- tile_count: int32 [4, 32], P('tm', 'ent'), may hold values from 1 to 8, as said below
- basis: bfloat16 [512, 2048], replicated, may hold values from -0.25 to 0.25
- coef: float32 [256, 4], replicated, may hold values from -3 to 3
- rel_emb: bfloat16 [256, 512], replicated, may hold values from -3 to 3
- self_weight: bfloat16 [512, 512], replicated, may hold values from -0.25 to 0.25
- gate_weight: bfloat16 [512, 512], replicated, may hold values from -0.25 to 0.25
- gate_bias: float32 [512], replicated, may hold values from -2 to 1
Outputs:
- grad_states: float32 [4, 32768, 512], P('tm', 'ent')
- grad_basis: float32 [512, 2048], P('ent')
- grad_self: float32 [512, 512], P('ent')
- grad_gate: float32 [512, 512], P('ent')
- grad_gate_bias: float32 [512], P('ent')
- grad_coef: float32 [256, 4], P('ent')
- grad_rel_emb: float32 [256, 512], P('ent')
Inputs may be any that keep to these rules, and one draw needn't show every extreme that they name: `tile_count`: some slab of some snapshot has 8 live tiles in every draw.
All inputs are finite; a program needn't handle non-finite values.
Results may differ from a plain program's by a relative error of at most 0.01.
Values may be sent and summed in bfloat16 or wider, within the bound.
A program may use at most 128 MiB of HBM per device.

v0:
```python
import jax
import jax.numpy as jnp
from jax import lax
from jax.sharding import PartitionSpec as P

TILE = 128


def shifted(block, axis, distance):
    devices = range(lax.axis_size(axis))
    route = [(i - distance, i) for i in devices if i - distance in devices]
    return lax.ppermute(block, axis, route)


def per_device(
    states,
    cotangent,
    export_rows,
    edge_src,
    edge_dst,
    edge_rel,
    tile_count,
    basis,
    coef,
    rel_emb,
    self_weight,
    gate_weight,
    gate_bias,
):
    ent_count = lax.axis_size("ent")
    section_count = lax.axis_size("tm")
    own_state = states[0]
    row_count, feature_width = own_state.shape
    basis_count = basis.shape[1] // feature_width
    relation_count = rel_emb.shape[0]
    exported_rows = export_rows[0]
    edge_source = edge_src[0]
    edge_target = edge_dst[0]
    edge_count = edge_source.shape[0]
    slot_count = exported_rows.shape[0]
    live_mask = jnp.arange(edge_count, dtype=jnp.int32) // TILE < tile_count[0, 0]
    rel_onehot = (
        edge_rel[0][:, None] == jnp.arange(relation_count, dtype=jnp.int32)[None, :]
    ).astype(jnp.float32)
    received = lax.all_to_all(
        own_state[exported_rows], "ent", split_axis=0, concat_axis=0, tiled=True
    )
    rel_rows = jnp.dot(rel_onehot.astype(jnp.bfloat16), rel_emb, preferred_element_type=jnp.float32)
    edge_input = (received[edge_source].astype(jnp.float32) + rel_rows).astype(jnp.bfloat16)
    images = jnp.dot(edge_input, basis, preferred_element_type=jnp.float32).reshape(
        edge_count, basis_count, feature_width
    )
    edge_coef = jnp.dot(rel_onehot, coef, precision=lax.Precision.HIGHEST)
    message = jnp.einsum("eb,ebd->ed", edge_coef, images)
    message = jnp.where(live_mask[:, None], message, jnp.zeros((), jnp.float32))
    degree = 1.0 + jax.ops.segment_sum(live_mask.astype(jnp.float32), edge_target, row_count)
    self_part = jnp.dot(own_state, self_weight, preferred_element_type=jnp.float32)
    summed = (jax.ops.segment_sum(message, edge_target, row_count) + self_part) / degree[:, None]
    aggregated = jnp.tanh(summed)
    gate_open = jax.nn.sigmoid(
        jnp.dot(own_state, gate_weight, preferred_element_type=jnp.float32) + gate_bias
    )
    state_float = own_state.astype(jnp.float32)
    handed = jnp.zeros((row_count, feature_width), jnp.bfloat16)
    contract_last = (((1,), (1,)), ((), ()))
    contract_first = (((0,), (0,)), ((), ()))
    for section_step in range(section_count):
        upstream = cotangent[0].astype(jnp.float32) + handed.astype(jnp.float32)
        row_grad = (
            upstream * gate_open * (1.0 - aggregated * aggregated) / degree[:, None]
        ).astype(jnp.bfloat16)
        gate_grad = upstream * (aggregated - state_float) * gate_open * (1.0 - gate_open)
        gate_row = gate_grad.astype(jnp.bfloat16)
        edge_grad = jnp.where(
            live_mask[:, None], row_grad[edge_target], jnp.zeros((), jnp.bfloat16)
        )
        image_grad = (
            (edge_coef[:, :, None] * edge_grad.astype(jnp.float32)[:, None, :])
            .astype(jnp.bfloat16)
            .reshape(edge_count, basis_count * feature_width)
        )
        input_grad = lax.dot_general(
            image_grad, basis, contract_last, preferred_element_type=jnp.float32
        )
        slot_grad = jax.ops.segment_sum(input_grad, edge_source, slot_count)
        returned = lax.all_to_all(slot_grad, "ent", split_axis=0, concat_axis=0, tiled=True)
        state_grad = upstream * (1.0 - gate_open)
        state_grad = state_grad + lax.dot_general(
            row_grad, self_weight, contract_last, preferred_element_type=jnp.float32
        )
        state_grad = state_grad + lax.dot_general(
            gate_row, gate_weight, contract_last, preferred_element_type=jnp.float32
        )
        state_grad = state_grad + jax.ops.segment_sum(returned, exported_rows, row_count)
        if section_step + 1 < section_count:
            handed = shifted(state_grad.astype(jnp.bfloat16), "tm", -1)
    basis_term = lax.dot_general(
        edge_input, image_grad, contract_first, preferred_element_type=jnp.float32
    )
    self_term = lax.dot_general(
        own_state, row_grad, contract_first, preferred_element_type=jnp.float32
    )
    gate_term = lax.dot_general(
        own_state, gate_row, contract_first, preferred_element_type=jnp.float32
    )
    bias_term = jnp.sum(gate_grad, axis=0)
    coef_edge = jnp.einsum("ed,ebd->eb", edge_grad.astype(jnp.float32), images)
    coef_term = lax.dot_general(
        rel_onehot, coef_edge, contract_first, precision=lax.Precision.HIGHEST
    )
    relation_term = lax.dot_general(
        rel_onehot, input_grad, contract_first, precision=lax.Precision.HIGHEST
    )
    summed_terms = lax.psum(
        (basis_term, self_term, gate_term, bias_term, coef_term, relation_term), ("tm", "ent")
    )
    slab_index = lax.axis_index("ent")
    final_parts = tuple(
        (
            lax.dynamic_slice_in_dim(
                matrix_term,
                slab_index * (matrix_term.shape[0] // ent_count),
                matrix_term.shape[0] // ent_count,
                0,
            )
            for matrix_term in summed_terms
        )
    )
    return (
        state_grad[None],
        final_parts[0],
        final_parts[1],
        final_parts[2],
        final_parts[3],
        final_parts[4],
        final_parts[5],
    )


def solution(mesh):
    placed = (
        P("tm", "ent", None),
        P("tm", "ent", None),
        P("tm", "ent"),
        P("tm", "ent"),
        P("tm", "ent"),
        P("tm", "ent"),
        P("tm", "ent"),
        P(),
        P(),
        P(),
        P(),
        P(),
        P(),
    )
    return jax.shard_map(
        per_device,
        mesh=mesh,
        in_specs=placed,
        out_specs=(
            P("tm", "ent", None),
            P("ent", None),
            P("ent", None),
            P("ent", None),
            P("ent"),
            P("ent", None),
            P("ent", None),
        ),
        check_vma=False,
    )
```

profile of v0, /device:TPU:64, one launch (start us, length us, event | category | flops | bytes accessed | tf_op | source)
XLA Modules:
  0.0 601.3 jit_solution(15642824185144486378)
XLA Ops:
  8.0 6.5 %gather_fusion = bf16[1024,512]{1,0:T(8,128)(2,1)} fusion(bf16[1024,512]{1,0:T(8,128)(2,1)} %bitcast.129, s32[1024]{0:T(1024)S(1)} %broadcast_clamp_fusion.2), kind=kCustom, calls=%fused_computation | custom fusion | bytes 2101248 | tf_op jit(solution)/shard_map/gather | solution.py:46
  14.6 7.6 %all-to-all-start = ((bf16[32,32,512]{2,1,0:T(8,128)(2,1)}), bf16[32,32,512]{2,1,0:T(8,128)(2,1)}, u32[]{:S(2)}, u32[]{:S(2)}) async-start(bf16[32,32,512]{2,1,0:T(8,128)(2,1)} %bitcast.140), calls=%async_computation | async-start | bytes 2097152 | tf_op jit(solution)/shard_map/all_to_all | solution.py:45
  25.8 7.8 %scatter_custom_fusion.1 = f32[1024]{0:T(1024)S(1)} fusion(s32[1024]{0:T(1024)S(1)} %bitcast.157, f32[1024]{0:T(1024)S(1)} %get-tuple-element.35, f32[]{:T(128)} %constant.14.clone.1), kind=kCustom, calls=%fused_computation.105 | custom fusion | flops 1024 | bytes 4100 | tf_op jit(solution)/shard_map/scatter-add | solution.py:56
  33.6 3.1 fusion.57
  36.7 2.2 all-to-all-done
  39.0 6.5 %gather_fusion.1 = bf16[1024,512]{1,0:T(8,128)(2,1)} fusion(bf16[1024,512]{1,0:T(8,128)(2,1)} %bitcast.10, s32[1024]{0:T(1024)S(1)} %broadcast_clamp_fusion.1), kind=kCustom, calls=%fused_computation.1 | custom fusion | bytes 2101248 | tf_op jit(solution)/shard_map/gather | solution.py:49
  48.2 4.3 fusion.64
  52.5 7.8 %reshape.211 = bf16[1024,4,512]{2,1,0:T(4,128)(2,1)} reshape(bf16[1024,2048]{1,0:T(8,128)(2,1)} %fusion.64) | data formatting | bytes 8388608 | tf_op jit(solution)/shard_map/reshape | solution.py:50
  60.4 6.0 fusion.65
  66.4 11.3 %scatter_custom_fusion = f32[1024,512]{1,0:T(8,128)} fusion(f32[1024,512]{1,0:T(8,128)} %fusion.57, s32[1024]{0:T(1024)S(1)} %bitcast.158, f32[1024,1,512]{2,1,0:T(1,128)} %fusion.65, f32[]{:T(128)} %constant.40.clone.1, pred[1024]{0:T(1024)(128)(4,1)S(1)} %get-tuple-element.34), kind=kCustom, calls=%fused_computation.35 | custom fusion | flops 1048576 | bytes 4195840 | tf_op jit(solution)/shard_map/scatter-add | solution.py:58
  77.7 5.2 fusion.4
  82.9 6.5 %gather_fusion.2 = bf16[1024,512]{1,0:T(8,128)(2,1)} fusion(bf16[1024,512]{1,0:T(8,128)(2,1)} %get-tuple-element.32, s32[1024]{0:T(1024)S(1)} %broadcast_clamp_fusion), kind=kCustom, calls=%fused_computation.2 | custom fusion | bytes 2101248 | tf_op jit(solution)/shard_map/gather | solution.py:75
  90.9 1.9 multiply_convert_fusion.3
  94.3 3.7 fusion.67
  98.0 8.7 %scatter_custom_fusion.2 = f32[1024,512]{1,0:T(8,128)} fusion(s32[1024]{0:T(1024)S(1)} %bitcast.159, f32[1024,512]{1,0:T(8,128)} %fusion.67, f32[]{:T(128)} %constant.40.clone.1), kind=kCustom, calls=%fused_computation.69 | custom fusion | flops 524288 | bytes 2097664 | tf_op jit(solution)/shard_map/scatter-add | solution.py:85
  106.7 5.7 all-to-all-start.1
  112.4 2.2 fusion.66
  114.8 4.1 fusion.1
  119.0 22.3 %all-to-all-done.1 = f32[32,32,512]{2,1,0:T(8,128)} async-done(((f32[32,32,512]{2,1,0:T(8,128)}), f32[32,32,512]{2,1,0:T(8,128)}, u32[]{:S(2)}, u32[]{:S(2)}) %all-to-all-start.1) | async-done | bytes 2097184 | tf_op jit(solution)/shard_map/all_to_all | solution.py:86
  141.3 10.2 %scatter_fusion = f32[1024,512]{1,0:T(8,128)} fusion(f32[1024,512]{1,0:T(8,128)} %fusion.1, s32[1024]{0:T(1024)S(1)} %bitcast.145, f32[1024,512]{1,0:T(8,128)} %bitcast.19), kind=kCustom, calls=%fused_computation.9 | custom fusion | flops 524288 | bytes 6295552 | tf_op jit(solution)/shard_map/scatter-add | solution.py:94
  151.5 1.9 convert_element_type.141
  153.4 2.0 collective-permute-start
  155.4 24.6 %collective-permute-done = bf16[1024,512]{1,0:T(8,128)(2,1)S(1)} collective-permute-done((bf16[1024,512]{1,0:T(8,128)(2,1)S(1)}, bf16[1024,512]{1,0:T(8,128)(2,1)S(1)}, u32[]{:S(2)}, u32[]{:S(2)}) %collective-permute-start) | collective-permute-done | bytes 1048608 | tf_op jit(solution)/shard_map/ppermute | solution.py:12
  181.0 3.5 divide_convert_fusion.2
  184.4 6.5 %gather_fusion.3 = bf16[1024,512]{1,0:T(8,128)(2,1)} fusion(bf16[1024,512]{1,0:T(8,128)(2,1)} %divide_convert_fusion.2, s32[1024]{0:T(1024)S(1)} %broadcast_clamp_fusion), kind=kCustom, calls=%fused_computation.3 | custom fusion | bytes 2101248 | tf_op jit(solution)/shard_map/gather | solution.py:75
  192.5 1.9 multiply_convert_fusion.2
  195.8 3.7 fusion.69
  199.5 8.7 %scatter_custom_fusion.4 = f32[1024,512]{1,0:T(8,128)} fusion(s32[1024]{0:T(1024)S(1)} %bitcast.160, f32[1024,512]{1,0:T(8,128)} %fusion.69, f32[]{:T(128)} %constant.40.clone.1), kind=kCustom, calls=%fused_computation.67 | custom fusion | flops 524288 | bytes 2097664 | tf_op jit(solution)/shard_map/scatter-add | solution.py:85
  208.2 4.9 all-to-all-start.2
  213.2 2.2 fusion.68
  215.6 4.9 add_add_fusion.2
  220.6 21.5 %all-to-all-done.2 = f32[32,32,512]{2,1,0:T(8,128)} async-done(((f32[32,32,512]{2,1,0:T(8,128)}), f32[32,32,512]{2,1,0:T(8,128)}, u32[]{:S(2)}, u32[]{:S(2)}) %all-to-all-start.2) | async-done | bytes 2097184 | tf_op jit(solution)/shard_map/all_to_all | solution.py:86
  242.0 10.2 %scatter_fusion.1 = f32[1024,512]{1,0:T(8,128)} fusion(f32[1024,512]{1,0:T(8,128)} %add_add_fusion.2, s32[1024]{0:T(1024)S(1)} %bitcast.146, f32[1024,512]{1,0:T(8,128)} %bitcast.21), kind=kCustom, calls=%fused_computation.11 | custom fusion | flops 524288 | bytes 6295552 | tf_op jit(solution)/shard_map/scatter-add | solution.py:94
  252.2 1.9 convert_element_type.148
  254.1 2.2 collective-permute-start.1
  256.3 24.4 %collective-permute-done.1 = bf16[1024,512]{1,0:T(8,128)(2,1)S(1)} collective-permute-done((bf16[1024,512]{1,0:T(8,128)(2,1)S(1)}, bf16[1024,512]{1,0:T(8,128)(2,1)S(1)}, u32[]{:S(2)}, u32[]{:S(2)}) %collective-permute-start.1) | collective-permute-done | bytes 1048608 | tf_op jit(solution)/shard_map/ppermute | solution.py:12
  281.7 3.5 divide_convert_fusion.1
  285.2 6.5 %gather_fusion.4 = bf16[1024,512]{1,0:T(8,128)(2,1)} fusion(bf16[1024,512]{1,0:T(8,128)(2,1)} %divide_convert_fusion.1, s32[1024]{0:T(1024)S(1)} %broadcast_clamp_fusion), kind=kCustom, calls=%fused_computation.4 | custom fusion | bytes 2101248 | tf_op jit(solution)/shard_map/gather | solution.py:75
  293.2 1.9 multiply_convert_fusion.1
  296.6 3.7 fusion.71
  300.3 8.7 %scatter_custom_fusion.6 = f32[1024,512]{1,0:T(8,128)} fusion(s32[1024]{0:T(1024)S(1)} %bitcast.161, f32[1024,512]{1,0:T(8,128)} %fusion.71, f32[]{:T(128)} %constant.40.clone.1), kind=kCustom, calls=%fused_computation.65 | custom fusion | flops 524288 | bytes 2097664 | tf_op jit(solution)/shard_map/scatter-add | solution.py:85
  309.0 4.8 all-to-all-start.3
  314.3 2.2 fusion.70
  316.7 4.9 add_add_fusion.1
  321.6 21.0 %all-to-all-done.3 = f32[32,32,512]{2,1,0:T(8,128)} async-done(((f32[32,32,512]{2,1,0:T(8,128)}), f32[32,32,512]{2,1,0:T(8,128)}, u32[]{:S(2)}, u32[]{:S(2)}) %all-to-all-start.3) | async-done | bytes 2097184 | tf_op jit(solution)/shard_map/all_to_all | solution.py:86
  342.7 10.2 %scatter_fusion.2 = f32[1024,512]{1,0:T(8,128)} fusion(f32[1024,512]{1,0:T(8,128)} %add_add_fusion.1, s32[1024]{0:T(1024)S(1)} %bitcast.147, f32[1024,512]{1,0:T(8,128)} %bitcast.23), kind=kCustom, calls=%fused_computation.13 | custom fusion | flops 524288 | bytes 6295552 | tf_op jit(solution)/shard_map/scatter-add | solution.py:94
  352.8 1.9 convert_element_type.155
  354.7 2.2 collective-permute-start.2
  356.9 24.4 %collective-permute-done.2 = bf16[1024,512]{1,0:T(8,128)(2,1)S(1)} collective-permute-done((bf16[1024,512]{1,0:T(8,128)(2,1)S(1)}, bf16[1024,512]{1,0:T(8,128)(2,1)S(1)}, u32[]{:S(2)}, u32[]{:S(2)}) %collective-permute-start.2) | collective-permute-done | bytes 1048608 | tf_op jit(solution)/shard_map/ppermute | solution.py:12
  381.3 4.3 fusion.63
  385.7 6.5 %gather_fusion.5 = bf16[1024,512]{1,0:T(8,128)(2,1)} fusion(bf16[1024,512]{1,0:T(8,128)(2,1)} %get-tuple-element.29, s32[1024]{0:T(1024)S(1)} %broadcast_clamp_fusion), kind=kCustom, calls=%fused_computation.5 | custom fusion | bytes 2101248 | tf_op jit(solution)/shard_map/gather | solution.py:75
  392.1 3.0 convolution_bitcast_fusion.1
  396.5 1.9 multiply_convert_fusion
  399.8 2.4 fusion.73
  402.2 4.5 fusion.74
  406.7 1.8 convolution_bitcast_fusion
  408.5 2.2 fusion.27
  410.7 8.8 %scatter_custom_fusion.8 = f32[1024,512]{1,0:T(8,128)} fusion(s32[1024]{0:T(1024)S(1)} %bitcast.162, f32[1024,512]{1,0:T(8,128)} %copy-done.26, f32[]{:T(128)} %constant.40.clone.1), kind=kCustom, calls=%fused_computation.63 | custom fusion | flops 524288 | bytes 2097664 | tf_op jit(solution)/shard_map/scatter-add | solution.py:85
  419.6 4.8 all-to-all-start.4
  424.4 6.4 %fusion.9 = f32[1024,1,4]{2,1,0:T(1,128)S(1)} fusion(bf16[1024,4,512]{2,1,0:T(4,128)(2,1)} %reshape.211, bf16[1024,512,1]{1,0,2:T(8,128)(2,1)} %get-tuple-element.30), kind=kOutput, calls=%fused_computation.36 | convolution fusion | flops 4194304 | bytes 5259264 | tf_op jit(solution)/shard_map/ed,ebd->eb/dot_general | solution.py:107
  431.5 78.4 %all-reduce = (f32[512]{0:T(512)S(1)}, f32[256,4]{0,1:T(4,128)S(1)}) all-reduce(f32[512]{0:T(512)S(1)} %get-tuple-element.27, f32[256,4]{0,1:T(4,128)S(1)} %fusion.28), channel_id=1, replica_groups=mesh['tm'=4,'ent'=32] {'tm','ent'}, use_global_device_ids=true, to_apply=%region_14.15 | all-reduce | flops 1536 | bytes 12288 | tf_op jit(solution)/shard_map/psum | solution.py:114
  513.0 3.8 add_add_fusion
  516.8 10.1 %scatter_fusion.3 = f32[1024,512]{1,0:T(8,128)} fusion(f32[1024,512]{1,0:T(8,128)} %add_add_fusion, s32[1024]{0:T(1024)S(1)} %bitcast.148, f32[1024,512]{1,0:T(8,128)} %bitcast.25), kind=kCustom, calls=%fused_computation.15 | custom fusion | flops 524288 | bytes 6295552 | tf_op jit(solution)/shard_map/scatter-add | solution.py:94
  526.9 60.9 %all-reduce.4.cloned.1.call-done = (f32[512,2048]{1,0:T(8,128)}, f32[512,512]{0,1:T(8,128)}, f32[512,512]{0,1:T(8,128)}, f32[256,512]{1,0:T(8,128)}) async-done(((f32[512,2048]{1,0:T(8,128)}, f32[512,512]{0,1:T(8,128)}, f32[512,512]{0,1:T(8,128)}, f32[256,512]{1,0:T(8,128)}), (f32[512,2048]{1,0:T(8,128)}, f32[512,512]{0,1:T(8,128)}, f32[512,512]{0,1:T(8,128)}, ...) | async-done | bytes 6815760 | tf_op jit(solution)/shard_map/psum | solution.py:114
  (112 shorter events, 31.2 us)
Async XLA Ops:
  7.2 41.0 %copy-start = (bf16[512,2048]{1,0:T(8,128)(2,1)S(1)}, bf16[512,2048]{1,0:T(8,128)(2,1)}, u32[]{:S(2)}) copy-start(bf16[512,2048]{1,0:T(8,128)(2,1)} %param.20) | copy-start | bytes 6291460
  14.5 8.3 %copy-start.36 = (s32[1,1024]{1,0:T(1,128)S(1)}, s32[1,1024]{1,0:T(1,128)}, u32[]{:S(2)}) copy-start(s32[1,1024]{1,0:T(1,128)} %param.17) | copy-start | bytes 12292
  14.5 8.3 %copy-start.35 = (s32[1,1024]{1,0:T(1,128)S(1)}, s32[1,1024]{1,0:T(1,128)}, u32[]{:S(2)}) copy-start(s32[1,1024]{1,0:T(1,128)} %param.18) | copy-start | bytes 12292
  14.5 8.3 %copy-start.38 = (f32[256,4]{0,1:T(4,128)S(1)}, f32[256,4]{0,1:T(4,128)}, u32[]{:S(2)}) copy-start(f32[256,4]{0,1:T(4,128)} %param.21) | copy-start | bytes 12292
  14.5 19.0 %copy-start.37 = (s32[1,1024]{1,0:T(1,128)S(1)}, s32[1,1024]{1,0:T(1,128)}, u32[]{:S(2)}) copy-start(s32[1,1024]{1,0:T(1,128)} %param.16) | copy-start | bytes 12292
  14.5 19.1 %copy-start.1 = (bf16[1,1024,512]{2,1,0:T(8,128)(2,1)S(1)}, bf16[1,1024,512]{2,1,0:T(8,128)(2,1)}, u32[]{:S(2)}) copy-start(bf16[1,1024,512]{2,1,0:T(8,128)(2,1)} %param.13) | copy-start | bytes 3145732
  14.6 24.4 %all-to-all-start = ((bf16[32,32,512]{2,1,0:T(8,128)(2,1)}), bf16[32,32,512]{2,1,0:T(8,128)(2,1)}, u32[]{:S(2)}, u32[]{:S(2)}) async-start(bf16[32,32,512]{2,1,0:T(8,128)(2,1)} %bitcast.140), calls=%async_computation | async-start | bytes 2097152 | tf_op jit(solution)/shard_map/all_to_all | solution.py:45
  38.9 6.5 %copy-start.33 = (bf16[256,512]{1,0:T(8,128)(2,1)S(1)}, bf16[256,512]{1,0:T(8,128)(2,1)}, u32[]{:S(2)}) copy-start(bf16[256,512]{1,0:T(8,128)(2,1)} %param.22) | copy-start | bytes 786436
  47.2 1.0 copy-start.21
  66.4 11.3 %copy-start.39 = (f32[512]{0:T(512)S(1)}, f32[512]{0:T(512)}, u32[]{:S(2)}) copy-start(f32[512]{0:T(512)} %param.25) | copy-start | bytes 6148
  89.4 1.5 copy-start.17
  106.7 34.6 %all-to-all-start.1 = ((f32[32,32,512]{2,1,0:T(8,128)}), f32[32,32,512]{2,1,0:T(8,128)}, u32[]{:S(2)}, u32[]{:S(2)}) async-start(f32[32,32,512]{2,1,0:T(8,128)} %bitcast.138), calls=%async_computation.1 | async-start | bytes 4194304 | tf_op jit(solution)/shard_map/all_to_all | solution.py:86
  112.4 2.3 copy-start.3
  112.4 2.3 copy-start.10
  112.4 2.4 copy-start.29
  114.8 26.4 %copy-start.34 = (s32[1,1024]{1,0:T(1,128)S(1)}, s32[1,1024]{1,0:T(1,128)}, u32[]{:S(2)}) copy-start(s32[1,1024]{1,0:T(1,128)} %param.15) | copy-start | bytes 12292
  151.5 29.5 %copy-start.4 = (f32[1024,512]{1,0:T(8,128)S(1)}, f32[1024,512]{1,0:T(8,128)}, u32[]{:S(2)}) copy-start(f32[1024,512]{1,0:T(8,128)} %get-tuple-element.33) | copy-start | bytes 6291460
  151.5 29.5 %copy-start.11 = (bf16[1,1024,512]{2,1,0:T(8,128)(2,1)S(1)}, bf16[1,1024,512]{2,1,0:T(8,128)(2,1)}, u32[]{:S(2)}) copy-start(bf16[1,1024,512]{2,1,0:T(8,128)(2,1)} %param.14) | copy-start | bytes 3145732
  153.4 26.6 %collective-permute-start = (bf16[1024,512]{1,0:T(8,128)(2,1)S(1)}, bf16[1024,512]{1,0:T(8,128)(2,1)S(1)}, u32[]{:S(2)}, u32[]{:S(2)}) collective-permute-start(bf16[1024,512]{1,0:T(8,128)(2,1)S(1)} %convert_element_type.141), channel_id=1, source_target_pairs={{32,0},{64,32},{96,64},{33,1},{65,33},{97,65},{34,2},{66,34},{98,6... | collective-permute-start | bytes 3145736 | tf_op jit(solution)/shard_map/ppermute | solution.py:12
  179.9 1.0 copy-start.28
  190.9 1.5 copy-start.18
  208.2 33.8 %all-to-all-start.2 = ((f32[32,32,512]{2,1,0:T(8,128)}), f32[32,32,512]{2,1,0:T(8,128)}, u32[]{:S(2)}, u32[]{:S(2)}) async-start(f32[32,32,512]{2,1,0:T(8,128)} %bitcast.139), calls=%async_computation.2 | async-start | bytes 4194304 | tf_op jit(solution)/shard_map/all_to_all | solution.py:86
  213.2 2.3 copy-start.5
  213.2 2.3 copy-start.12
  213.2 2.4 copy-start.30
  252.2 29.5 %copy-start.6 = (f32[1024,512]{1,0:T(8,128)S(1)}, f32[1024,512]{1,0:T(8,128)}, u32[]{:S(2)}) copy-start(f32[1024,512]{1,0:T(8,128)} %get-tuple-element.33) | copy-start | bytes 6291460
  252.2 29.5 %copy-start.13 = (bf16[1,1024,512]{2,1,0:T(8,128)(2,1)S(1)}, bf16[1,1024,512]{2,1,0:T(8,128)(2,1)}, u32[]{:S(2)}) copy-start(bf16[1,1024,512]{2,1,0:T(8,128)(2,1)} %param.14) | copy-start | bytes 3145732
  254.1 26.6 %collective-permute-start.1 = (bf16[1024,512]{1,0:T(8,128)(2,1)S(1)}, bf16[1024,512]{1,0:T(8,128)(2,1)S(1)}, u32[]{:S(2)}, u32[]{:S(2)}) collective-permute-start(bf16[1024,512]{1,0:T(8,128)(2,1)S(1)} %convert_element_type.148), channel_id=1, source_target_pairs={{32,0},{64,32},{96,64},{33,1},{65,33},{97,65},{34,2},{66,34},{98,6... | collective-permute-start | bytes 3145736 | tf_op jit(solution)/shard_map/ppermute | solution.py:12
  280.7 1.0 copy-start.27
  291.7 1.5 copy-start.19
  309.0 33.6 %all-to-all-start.3 = ((f32[32,32,512]{2,1,0:T(8,128)}), f32[32,32,512]{2,1,0:T(8,128)}, u32[]{:S(2)}, u32[]{:S(2)}) async-start(f32[32,32,512]{2,1,0:T(8,128)} %bitcast.137), calls=%async_computation.3 | async-start | bytes 4194304 | tf_op jit(solution)/shard_map/all_to_all | solution.py:86
  313.8 274.0 %all-reduce.4.cloned.1.call-start = ((), (), s32[]{:S(2)}) async-start(), calls=%async_computation.5 | async-start | bytes 13631488 | tf_op jit(solution)/shard_map/psum | solution.py:114
  314.2 2.3 copy-start.7
  314.2 2.3 copy-start.14
  314.3 2.4 copy-start.31
  352.8 28.5 %copy-start.8 = (f32[1024,512]{1,0:T(8,128)S(1)}, f32[1024,512]{1,0:T(8,128)}, u32[]{:S(2)}) copy-start(f32[1024,512]{1,0:T(8,128)} %get-tuple-element.33) | copy-start | bytes 6291460
  352.8 28.5 %copy-start.15 = (bf16[1,1024,512]{2,1,0:T(8,128)(2,1)S(1)}, bf16[1,1024,512]{2,1,0:T(8,128)(2,1)}, u32[]{:S(2)}) copy-start(bf16[1,1024,512]{2,1,0:T(8,128)(2,1)} %param.14) | copy-start | bytes 3145732
  354.7 26.6 %collective-permute-start.2 = (bf16[1024,512]{1,0:T(8,128)(2,1)S(1)}, bf16[1024,512]{1,0:T(8,128)(2,1)S(1)}, u32[]{:S(2)}, u32[]{:S(2)}) collective-permute-start(bf16[1024,512]{1,0:T(8,128)(2,1)S(1)} %convert_element_type.155), channel_id=1, source_target_pairs={{32,0},{64,32},{96,64},{33,1},{65,33},{97,65},{34,2},{66,34},{98,6... | collective-permute-start | bytes 3145736 | tf_op jit(solution)/shard_map/ppermute | solution.py:12
  381.3 4.3 copy-start.23
  392.1 3.1 copy-start.25
  395.2 1.3 copy-start.20
  399.8 2.4 copy-start.22
  402.2 6.3 %copy-start.26 = (f32[1024,512]{1,0:T(8,128)}, f32[1024,512]{1,0:T(8,128)S(1)}, u32[]{:S(2)}) copy-start(f32[1024,512]{1,0:T(8,128)S(1)} %fusion.73) | copy-start | bytes 6291460
  402.2 4.5 copy-start.24
  419.6 97.2 %all-to-all-start.4 = ((f32[32,32,512]{2,1,0:T(8,128)}), f32[32,32,512]{2,1,0:T(8,128)}, u32[]{:S(2)}, u32[]{:S(2)}) async-start(f32[32,32,512]{2,1,0:T(8,128)} %bitcast.136), calls=%async_computation.4 | async-start | bytes 4194304 | tf_op jit(solution)/shard_map/all_to_all | solution.py:86
  424.3 86.8 %copy-start.2 = (bf16[1024,512]{1,0:T(8,128)(2,1)S(1)}, bf16[1024,512]{1,0:T(8,128)(2,1)}, u32[]{:S(2)}) copy-start(bf16[1024,512]{1,0:T(8,128)(2,1)} %get-tuple-element.29) | copy-start | bytes 3145732
  509.9 3.0 copy-start.9
  509.9 3.0 copy-start.16
  509.9 3.0 copy-start.32
Sparse Core Ops, SparseCore 0:
  410.8 176.9 all-reduce.3
where the time goes:
time: 608 us; the launch traced here: 601 us
  waiting for transfers between devices  201 us (33%)
  other arithmetic  126 us (21%)
  matrix products  79.3 us (13%)
  blocking collectives  78.4 us (13%)
  local copies, waits for them, and re-layouts  66.1 us (11%)
  starting transfers between devices  34.6 us (6%)
  between operations  15.4 us (3%)
    psum x1, blocking collectives, per_device(): lax.psum((basis_term, self_term, gate_term, bias_term, coef_term, relatio...  78.4 us
    ppermute x3, waiting for transfers between devices, shifted(): return lax.ppermute(block, axis, route)  73.3 us
    all_to_all x4, waiting for transfers between devices, per_device(): lax.all_to_all(slot_grad, 'ent', split_axis=0, concat_axis=0, tiled=True)  64.8 us
    psum x1, waiting for transfers between devices, per_device(): lax.psum((basis_term, self_term, gate_term, bias_term, coef_term, relatio...  60.9 us
    scatter-add x4, other arithmetic, per_device(): jax.ops.segment_sum(returned, exported_rows, row_count)  40.7 us
    scatter-add x4, other arithmetic, per_device(): slot_grad = jax.ops.segment_sum(input_grad, edge_source, slot_count)  35 us
    gather x4, local copies, waits for them, and re-layouts, per_device(): row_grad[edge_target]  26 us
    all_to_all x4, starting transfers between devices, per_device(): lax.all_to_all(slot_grad, 'ent', split_axis=0, concat_axis=0, tiled=True)  20.2 us
  transfers between devices with their start and end apart: 9, of which 8 were waited for; matrix products, arithmetic and copies ran while one was open for 11% of the time, Pallas kernels for 0%

commit v1 on v0

v1 whole, which is shorter than its diff:
```python
import jax
import jax.numpy as jnp
from jax import lax
from jax.sharding import PartitionSpec as P

TILE = 128
LAST = (((1,), (1,)), ((), ()))
FIRST = (((0,), (0,)), ((), ()))


def shifted(block, axis, distance):
    devices = range(lax.axis_size(axis))
    route = [(i - distance, i) for i in devices if i - distance in devices]
    return lax.ppermute(block, axis, route)


def dot(a, b, dims=(((1,), (0,)), ((), ()))):
    return lax.dot_general(a, b, dims, preferred_element_type=jnp.float32)


def onehot(ids, count):
    return ids[:, None] == jnp.arange(count, dtype=jnp.int32)[None, :]


def split_dot(hot, value):
    high = value.astype(jnp.bfloat16)
    low = (value - high.astype(jnp.float32)).astype(jnp.bfloat16)
    return dot(hot, high, FIRST) + dot(hot, low, FIRST)


def per_device(
    states, cotangent, export_rows, edge_src, edge_dst, edge_rel, tile_count,
    basis, coef, rel_emb, self_weight, gate_weight, gate_bias,
):
    bf16, f32 = jnp.bfloat16, jnp.float32
    ent_count = lax.axis_size("ent")
    section_count = lax.axis_size("tm")
    state = states[0]
    rows, width = state.shape
    basis_count = basis.shape[1] // width
    relations = rel_emb.shape[0]
    edges = edge_src.shape[1]
    slots = export_rows.shape[1]
    live = jnp.arange(edges, dtype=jnp.int32) // TILE < tile_count[0, 0]
    source = onehot(edge_src[0], slots).astype(bf16)
    target = (onehot(edge_dst[0], rows) & live[:, None]).astype(bf16)
    exported = onehot(export_rows[0], rows).astype(bf16)
    relation = onehot(edge_rel[0], relations).astype(bf16)

    received = lax.all_to_all(
        dot(exported, state).astype(bf16), "ent", split_axis=0, concat_axis=0, tiled=True
    )
    edge_input = (dot(source, received) + dot(relation, rel_emb)).astype(bf16)
    coef_high = coef.astype(bf16)
    coef_rest = coef - coef_high.astype(f32)
    coef_mid = coef_rest.astype(bf16)
    coef_low = (coef_rest - coef_mid.astype(f32)).astype(bf16)
    edge_coef = dot(relation, coef_high) + dot(relation, coef_mid) + dot(relation, coef_low)
    images = [
        dot(edge_input, basis[:, b * width : (b + 1) * width]) for b in range(basis_count)
    ]
    message = sum(edge_coef[:, b : b + 1] * images[b] for b in range(basis_count))
    degree = 1.0 + jnp.sum(target.astype(f32), axis=0)
    self_part = dot(state, self_weight)
    summed = (split_dot(target, message) + self_part) / degree[:, None]
    aggregated = jnp.tanh(summed)
    gate_open = jax.nn.sigmoid(dot(state, gate_weight) + gate_bias)
    keep = 1.0 - gate_open
    row_factor = gate_open * (1.0 - aggregated * aggregated) / degree[:, None]
    gate_factor = (aggregated - state.astype(f32)) * gate_open * keep

    handed = jnp.zeros((rows, width), bf16)
    for step in range(section_count):
        upstream = cotangent[0].astype(f32) + handed.astype(f32)
        row_grad = (upstream * row_factor).astype(bf16)
        gate_grad = upstream * gate_factor
        gate_row = gate_grad.astype(bf16)
        edge_grad = dot(target, row_grad)
        image_grad = [
            (edge_coef[:, b : b + 1] * edge_grad).astype(bf16) for b in range(basis_count)
        ]
        input_grad = sum(
            dot(image_grad[b], basis[:, b * width : (b + 1) * width], LAST)
            for b in range(basis_count)
        )
        slot_grad = dot(source, input_grad.astype(bf16), FIRST).astype(bf16)
        returned = lax.all_to_all(slot_grad, "ent", split_axis=0, concat_axis=0, tiled=True)
        state_grad = (
            upstream * keep
            + dot(row_grad, self_weight, LAST)
            + dot(gate_row, gate_weight, LAST)
            + dot(exported, returned, FIRST)
        )
        if step + 1 < section_count:
            handed = shifted(state_grad.astype(bf16), "tm", -1)

    coef_edge = jnp.stack(
        [jnp.sum(edge_grad * images[b], axis=1) for b in range(basis_count)], axis=1
    )
    small = jnp.concatenate(
        [
            jnp.sum(gate_grad, axis=0).reshape(ent_count, 1, width // ent_count),
            split_dot(relation, coef_edge).reshape(ent_count, 1, -1),
        ],
        axis=2,
    )
    small_width = small.shape[2]
    terms = [dot(edge_input, image_grad[b], FIRST) for b in range(basis_count)]
    terms += [dot(state, row_grad, FIRST), dot(state, gate_row, FIRST)]
    terms += [split_dot(relation, input_grad)]
    packed = jnp.concatenate(
        [term.reshape(ent_count, -1, width) for term in terms]
        + [jnp.pad(small, ((0, 0), (0, 7), (0, width - small_width)))],
        axis=1,
    )
    share = lax.psum_scatter(packed, "ent", scatter_dimension=0, tiled=False)
    share = lax.psum(share, "tm")
    height = width // ent_count
    top = basis_count * height
    return (
        state_grad[None],
        jnp.concatenate([share[b * height : (b + 1) * height] for b in range(basis_count)], axis=1),
        share[top : top + height],
        share[top + height : top + 2 * height],
        share[-8, :height],
        share[-8, height:small_width].reshape(relations // ent_count, basis_count),
        share[top + 2 * height : -8],
    )


def solution(mesh):
    placed = (P("tm", "ent", None),) * 2 + (P("tm", "ent"),) * 5 + (P(),) * 6
    return jax.shard_map(
        per_device,
        mesh=mesh,
        in_specs=placed,
        out_specs=(
            P("tm", "ent", None),
            P("ent", None),
            P("ent", None),
            P("ent", None),
            P("ent"),
            P("ent", None),
            P("ent", None),
        ),
        check_vma=False,
    )
```

time: 608 us -> 438 us (0.72)
  other arithmetic: 126 us -> 3.5 us
  blocking collectives: 78.4 us -> 0 us
  local copies, waits for them, and re-layouts: 66.1 us -> 19.6 us
  matrix products: 79.3 us -> 123 us
  waiting for transfers between devices: 201 us -> 237 us
    scatter-add x10 -> x0, other arithmetic: 94.7 us -> none  [the longest x4 40.7 us: per_device(): jax.ops.segment_sum(returned, exported_rows, row_count)]
    psum x1 -> x0, blocking collectives: 78.4 us -> none  [per_device(): lax.psum((basis_term, self_term, gate_term, bias_term, coef_term, relatio...]
    reduce_scatter x0 -> x1, waiting for transfers between devices: none -> 56.1 us  [per_device(): share = lax.psum_scatter(packed, 'ent', scatter_dimension=0, tiled=False)]
    dot_general x24 -> x57, matrix products: 79.3 us -> 123 us  [dot(): return lax.dot_general(a, b, dims, preferred_element_type=jnp.float32)]
    gather x6 -> x0, local copies, waits for them, and re-layouts: 39 us -> none  [the longest x4 26 us: per_device(): row_grad[edge_target]]
    convert_element_type x12 -> x2, other arithmetic: 24.9 us -> 0.89 us  [per_device(): row_grad = (upstream * row_factor).astype(bf16)]
    psum x1, waiting for transfers between devices: 60.9 us -> 37.2 us  [per_device(): share = lax.psum(share, 'tm')]
    all_to_all x1, waiting for transfers between devices: 2.24 us -> 14 us  [per_device(): lax.all_to_all(dot(exported, state).astype(bf16), 'ent', split_axis=0, co...]
  transfers between devices with their start and end apart: 9 -> 10, of which waited for: 8 -> 10; matrix products, arithmetic and copies ran while one was open for 11% -> 7% of each run, Pallas kernels for 0% -> 0%
where the time goes in v1:
time: 438 us; the launch traced here: 432 us
  waiting for transfers between devices  237 us (54%)
  matrix products  123 us (28%)
  starting transfers between devices  33.4 us (8%)
  local copies, waits for them, and re-layouts  19.6 us (4%)
  between operations  15.6 us (4%)
    dot_general x57, matrix products, dot(): return lax.dot_general(a, b, dims, preferred_element_type=jnp.float32)  123 us
    ppermute x3, waiting for transfers between devices, shifted(): return lax.ppermute(block, axis, route)  75.4 us
    reduce_scatter x1, waiting for transfers between devices, per_device(): share = lax.psum_scatter(packed, 'ent', scatter_dimension=0, tiled=False)  56.1 us
    all_to_all x4, waiting for transfers between devices, per_device(): lax.all_to_all(slot_grad, 'ent', split_axis=0, concat_axis=0, tiled=True)  54.7 us
    psum x1, waiting for transfers between devices, per_device(): share = lax.psum(share, 'tm')  37.2 us
    all_to_all x4, starting transfers between devices, per_device(): lax.all_to_all(slot_grad, 'ent', split_axis=0, concat_axis=0, tiled=True)  19 us
    all_to_all x1, waiting for transfers between devices, per_device(): lax.all_to_all(dot(exported, state).astype(bf16), 'ent', split_axis=0, co...  14 us
    unnamed x121, local copies, waits for them, and re-layouts  13.5 us
  transfers between devices with their start and end apart: 10, of which 10 were waited for; matrix products, arithmetic and copies ran while one was open for 7% of the time, Pallas kernels for 0%

profile of v1, /device:TPU:64, one launch (start us, length us, event | category | flops | bytes accessed | tf_op | source)
XLA Modules:
  0.0 432.4 jit_solution(14376339186520833855)
XLA Ops:
  7.2 3.6 fusion.57
  10.8 7.5 %all-to-all-start = ((bf16[32,32,512]{2,1,0:T(8,128)(2,1)}), bf16[32,32,512]{2,1,0:T(8,128)(2,1)S(1)}, u32[]{:S(2)}, u32[]{:S(2)}) async-start(bf16[32,32,512]{2,1,0:T(8,128)(2,1)} %bitcast.9), calls=%async_computation | async-start | bytes 2097152 | tf_op jit(solution)/shard_map/all_to_all | solution.py:50
  18.9 1.1 convert_reduce_fusion
  21.1 14.0 %all-to-all-done = bf16[32,32,512]{2,1,0:T(8,128)(2,1)S(1)} async-done(((bf16[32,32,512]{2,1,0:T(8,128)(2,1)}), bf16[32,32,512]{2,1,0:T(8,128)(2,1)S(1)}, u32[]{:S(2)}, u32[]{:S(2)}) %all-to-all-start) | async-done | bytes 1048608 | tf_op jit(solution)/shard_map/all_to_all | solution.py:50
  35.1 1.3 fusion.9
  40.3 2.4 multiply_add_fusion
  42.7 1.6 fusion.22
  44.4 1.6 fusion.20
  46.9 3.4 multiply_multiply_fusion
  50.4 1.7 fusion.13
  52.1 2.3 fusion.62
  54.4 2.1 fusion.60
  56.5 2.1 fusion.61
  58.6 6.9 %fusion.53 = bf16[1024,512]{1,0:T(8,128)(2,1)} fusion(s32[1024]{0:T(1024)S(1)} %bitcast.178, f32[1024,512]{1,0:T(8,128)} %fusion.62, f32[1024,512]{1,0:T(8,128)} %fusion.60, f32[1024,512]{1,0:T(8,128)} %fusion.61, f32[1024,512]{0,1:T(8,128)} %copy-done.24, f32[1024]{0:T(1024)S(1)} %bitcast.148, bf16[512,2048]{1,0:T(8,128)(2,1)} %param.20), kind=kOutput, calls=%fused_computation.97 | convolution fusion | flops 1615331328 | bytes 9969664 | tf_op jit(solution)/shard_map/dot_general | solution.py:18
  65.4 4.7 %all-to-all-start.1 = ((bf16[32,32,512]{2,1,0:T(8,128)(2,1)}), bf16[32,32,512]{2,1,0:T(8,128)(2,1)}, u32[]{:S(2)}, u32[]{:S(2)}) async-start(bf16[32,32,512]{2,1,0:T(8,128)(2,1)} %bitcast.126), calls=%async_computation.1 | async-start | bytes 2097152 | tf_op jit(solution)/shard_map/all_to_all | solution.py:87
  70.1 3.7 fusion.158
  73.8 13.1 %all-to-all-done.1 = bf16[32,32,512]{2,1,0:T(8,128)(2,1)} async-done(((bf16[32,32,512]{2,1,0:T(8,128)(2,1)}), bf16[32,32,512]{2,1,0:T(8,128)(2,1)}, u32[]{:S(2)}, u32[]{:S(2)}) %all-to-all-start.1) | async-done | bytes 1048608 | tf_op jit(solution)/shard_map/all_to_all | solution.py:87
  86.9 2.9 fusion.3
  90.9 2.0 collective-permute-start
  93.0 25.3 %collective-permute-done = bf16[1024,512]{1,0:T(8,128)(2,1)S(1)} collective-permute-done((bf16[1024,512]{1,0:T(8,128)(2,1)S(1)}, bf16[1024,512]{1,0:T(8,128)(2,1)S(1)}, u32[]{:S(2)}, u32[]{:S(2)}) %collective-permute-start) | collective-permute-done | bytes 1048608 | tf_op jit(solution)/shard_map/ppermute | solution.py:14
  119.2 2.6 fusion.11
  121.9 2.1 fusion.66
  124.0 2.1 fusion.64
  126.1 2.1 fusion.65
  128.2 6.9 %fusion.54 = bf16[1024,512]{1,0:T(8,128)(2,1)} fusion(s32[1024]{0:T(1024)S(1)} %bitcast.179, f32[1024,512]{1,0:T(8,128)} %fusion.66, f32[1024,512]{1,0:T(8,128)} %fusion.64, f32[1024,512]{1,0:T(8,128)} %fusion.65, f32[1024,512]{0,1:T(8,128)} %copy-done.25, f32[1024]{0:T(1024)S(1)} %bitcast.149, bf16[512,2048]{1,0:T(8,128)(2,1)} %param.20), kind=kOutput, calls=%fused_computation.98 | convolution fusion | flops 1615331328 | bytes 9969664 | tf_op jit(solution)/shard_map/dot_general | solution.py:18
  135.0 4.7 %all-to-all-start.2 = ((bf16[32,32,512]{2,1,0:T(8,128)(2,1)}), bf16[32,32,512]{2,1,0:T(8,128)(2,1)}, u32[]{:S(2)}, u32[]{:S(2)}) async-start(bf16[32,32,512]{2,1,0:T(8,128)(2,1)} %bitcast.125), calls=%async_computation.2 | async-start | bytes 2097152 | tf_op jit(solution)/shard_map/all_to_all | solution.py:87
  139.7 3.3 fusion.162
  143.0 13.5 %all-to-all-done.2 = bf16[32,32,512]{2,1,0:T(8,128)(2,1)} async-done(((bf16[32,32,512]{2,1,0:T(8,128)(2,1)}), bf16[32,32,512]{2,1,0:T(8,128)(2,1)}, u32[]{:S(2)}, u32[]{:S(2)}) %all-to-all-start.2) | async-done | bytes 1048608 | tf_op jit(solution)/shard_map/all_to_all | solution.py:87
  156.5 3.0 fusion.2
  160.9 2.2 collective-permute-start.1
  163.2 25.1 %collective-permute-done.1 = bf16[1024,512]{1,0:T(8,128)(2,1)S(1)} collective-permute-done((bf16[1024,512]{1,0:T(8,128)(2,1)S(1)}, bf16[1024,512]{1,0:T(8,128)(2,1)S(1)}, u32[]{:S(2)}, u32[]{:S(2)}) %collective-permute-start.1) | collective-permute-done | bytes 1048608 | tf_op jit(solution)/shard_map/ppermute | solution.py:14
  189.2 2.4 fusion.15
  191.7 2.1 fusion.70
  193.8 2.1 fusion.68
  195.9 2.1 fusion.69
  197.9 6.9 %fusion.55 = bf16[1024,512]{1,0:T(8,128)(2,1)} fusion(s32[1024]{0:T(1024)S(1)} %bitcast.180, f32[1024,512]{1,0:T(8,128)} %fusion.70, f32[1024,512]{1,0:T(8,128)} %fusion.68, f32[1024,512]{1,0:T(8,128)} %fusion.69, f32[1024,512]{0,1:T(8,128)} %copy-done.26, f32[1024]{0:T(1024)S(1)} %bitcast.150, bf16[512,2048]{1,0:T(8,128)(2,1)} %param.20), kind=kOutput, calls=%fused_computation.99 | convolution fusion | flops 1615331328 | bytes 9969664 | tf_op jit(solution)/shard_map/dot_general | solution.py:18
  204.8 4.7 %all-to-all-start.3 = ((bf16[32,32,512]{2,1,0:T(8,128)(2,1)}), bf16[32,32,512]{2,1,0:T(8,128)(2,1)}, u32[]{:S(2)}, u32[]{:S(2)}) async-start(bf16[32,32,512]{2,1,0:T(8,128)(2,1)} %bitcast.124), calls=%async_computation.3 | async-start | bytes 2097152 | tf_op jit(solution)/shard_map/all_to_all | solution.py:87
  209.5 3.3 fusion.163
  212.8 13.4 %all-to-all-done.3 = bf16[32,32,512]{2,1,0:T(8,128)(2,1)} async-done(((bf16[32,32,512]{2,1,0:T(8,128)(2,1)}), bf16[32,32,512]{2,1,0:T(8,128)(2,1)}, u32[]{:S(2)}, u32[]{:S(2)}) %all-to-all-start.3) | async-done | bytes 1048608 | tf_op jit(solution)/shard_map/all_to_all | solution.py:87
  226.2 3.0 fusion.1
  230.7 2.6 collective-permute-start.2
  233.4 25.0 %collective-permute-done.2 = bf16[1024,512]{1,0:T(8,128)(2,1)S(1)} collective-permute-done((bf16[1024,512]{1,0:T(8,128)(2,1)S(1)}, bf16[1024,512]{1,0:T(8,128)(2,1)S(1)}, u32[]{:S(2)}, u32[]{:S(2)}) %collective-permute-start.2) | collective-permute-done | bytes 1048608 | tf_op jit(solution)/shard_map/ppermute | solution.py:14
  259.5 3.8 multiply_reduce_fusion.3
  266.4 1.8 fusion.111
  268.1 1.7 fusion.113
  269.9 1.8 fusion.115
  271.6 1.7 fusion.74
  274.4 1.7 fusion.72
  276.9 1.3 copy-done.16
  278.2 1.5 fusion.95
  280.8 2.4 constant_dynamic-update-slice_fusion.4
  284.2 1.1 constant_dynamic-update-slice_fusion.2
  287.5 1.5 fusion.59
  290.1 4.2 fusion.56
  294.2 5.0 %all-to-all-start.4 = ((bf16[32,32,512]{2,1,0:T(8,128)(2,1)}), bf16[32,32,512]{2,1,0:T(8,128)(2,1)}, u32[]{:S(2)}, u32[]{:S(2)}) async-start(bf16[32,32,512]{2,1,0:T(8,128)(2,1)} %bitcast.127), calls=%async_computation.4 | async-start | bytes 2097152 | tf_op jit(solution)/shard_map/all_to_all | solution.py:87
  299.3 2.0 fusion.164
  301.4 14.7 %all-to-all-done.4 = bf16[32,32,512]{2,1,0:T(8,128)(2,1)} async-done(((bf16[32,32,512]{2,1,0:T(8,128)(2,1)}), bf16[32,32,512]{2,1,0:T(8,128)(2,1)}, u32[]{:S(2)}, u32[]{:S(2)}) %all-to-all-start.4) | async-done | bytes 1048608 | tf_op jit(solution)/shard_map/all_to_all | solution.py:87
  316.1 4.3 fusion
  320.3 56.1 %reduce-scatter.2.cloned.1.call-done = f32[1,112,512]{2,1,0:T(8,128)} async-done(((f32[32,112,512]{2,1,0:T(8,128)}), f32[1,112,512]{2,1,0:T(8,128)}) %reduce-scatter.2.cloned.1.call-update) | async-done | bytes 229392 | tf_op jit(solution)/shard_map/reduce_scatter | solution.py:116
  376.5 5.4 %add_bitcast_fusion = f32[1,1024,512]{2,1,0:T(8,128)} fusion(f32[1024,512]{1,0:T(8,128)} %fusion, f32[1024,512]{1,0:T(8,128)} %fusion.164, bf16[1024,512]{1,0:T(8,128)(2,1)S(1)} %copy-done.35, f32[1024,512]{1,0:T(8,128)} %get-tuple-element.49, bf16[1,1024,512]{2,1,0:T(8,128)(2,1)S(1)} %copy-done.1, bf16[1024,512]{1,0:T(8,128)(2,1)} %copy-done.36, ...), kind=kOutput, calls=%fused_computation.39 | convolution fusion | flops 541065216 | bytes 12058624 | tf_op jit(solution)/shard_map/dot_general | solution.py:18
  381.9 37.2 %all-reduce.3.cloned.1.call-done = f32[112,512]{1,0:T(8,128)} async-done(((f32[112,512]{1,0:T(8,128)}), f32[112,512]{1,0:T(8,128)}) %all-reduce.3.cloned.1.call-update) | async-done | bytes 229392 | tf_op jit(solution)/shard_map/psum | solution.py:117
  420.6 1.5 fusion.160
  422.8 1.2 slice_bitcast_fusion
  424.0 1.3 slice.112
  (154 shorter events, 25.4 us)
Async XLA Ops:
  7.2 39.7 %copy-start = (bf16[512,512]{1,0:T(8,128)(2,1)S(1)}, bf16[512,512]{1,0:T(8,128)(2,1)}, u32[]{:S(2)}) copy-start(bf16[512,512]{1,0:T(8,128)(2,1)} %param.24) | copy-start | bytes 1572868
  10.8 8.1 %copy-start.50 = (s32[1,1024]{1,0:T(1,128)S(1)}, s32[1,1024]{1,0:T(1,128)}, u32[]{:S(2)}) copy-start(s32[1,1024]{1,0:T(1,128)} %param.17) | copy-start | bytes 12292
  10.8 9.3 %copy-start.49 = (s32[1,1024]{1,0:T(1,128)S(1)}, s32[1,1024]{1,0:T(1,128)}, u32[]{:S(2)}) copy-start(s32[1,1024]{1,0:T(1,128)} %param.18) | copy-start | bytes 12292
  10.8 9.3 %copy-start.53 = (f32[256,4]{0,1:T(4,128)S(1)}, f32[256,4]{0,1:T(4,128)}, u32[]{:S(2)}) copy-start(f32[256,4]{0,1:T(4,128)} %param.21) | copy-start | bytes 12292
  10.8 24.3 %copy-start.54 = (s32[1,1024]{1,0:T(1,128)S(1)}, s32[1,1024]{1,0:T(1,128)}, u32[]{:S(2)}) copy-start(s32[1,1024]{1,0:T(1,128)} %param.16) | copy-start | bytes 12292
  10.8 24.3 %all-to-all-start = ((bf16[32,32,512]{2,1,0:T(8,128)(2,1)}), bf16[32,32,512]{2,1,0:T(8,128)(2,1)S(1)}, u32[]{:S(2)}, u32[]{:S(2)}) async-start(bf16[32,32,512]{2,1,0:T(8,128)(2,1)} %bitcast.9), calls=%async_computation | async-start | bytes 2097152 | tf_op jit(solution)/shard_map/all_to_all | solution.py:50
  35.1 1.3 copy-start.48
  36.4 1.6 copy-start.2
  38.7 1.6 copy-start.18
  39.5 3.2 copy-start.20
  40.3 2.4 copy-start.22
  44.4 1.7 copy-start.31
  44.4 1.7 copy-start.51
  46.9 3.4 copy-start.1
  50.4 1.7 copy-start.6
  52.1 4.4 %copy-start.24 = (f32[1024,512]{0,1:T(8,128)}, f32[1024,512]{0,1:T(8,128)S(1)}, u32[]{:S(2)}) copy-start(f32[1024,512]{0,1:T(8,128)S(1)} %fusion.13) | copy-start | bytes 6291460
  65.4 21.4 %all-to-all-start.1 = ((bf16[32,32,512]{2,1,0:T(8,128)(2,1)}), bf16[32,32,512]{2,1,0:T(8,128)(2,1)}, u32[]{:S(2)}, u32[]{:S(2)}) async-start(bf16[32,32,512]{2,1,0:T(8,128)(2,1)} %bitcast.126), calls=%async_computation.1 | async-start | bytes 2097152 | tf_op jit(solution)/shard_map/all_to_all | solution.py:87
  70.1 16.8 %copy-start.55 = (s32[1,1024]{1,0:T(1,128)S(1)}, s32[1,1024]{1,0:T(1,128)}, u32[]{:S(2)}) copy-start(s32[1,1024]{1,0:T(1,128)} %param.15) | copy-start | bytes 12292
  86.9 3.0 copy-start.10
  86.9 3.0 copy-start.13
  86.9 3.2 copy-start.33
  90.0 28.2 %copy-start.7 = (f32[1024,512]{1,0:T(8,128)S(1)}, f32[1024,512]{1,0:T(8,128)}, u32[]{:S(2)}) copy-start(f32[1024,512]{1,0:T(8,128)} %copy-done.6) | copy-start | bytes 6291460
  90.9 27.3 %collective-permute-start = (bf16[1024,512]{1,0:T(8,128)(2,1)S(1)}, bf16[1024,512]{1,0:T(8,128)(2,1)S(1)}, u32[]{:S(2)}, u32[]{:S(2)}) collective-permute-start(bf16[1024,512]{1,0:T(8,128)(2,1)S(1)} %fusion.27), channel_id=1, source_target_pairs={{32,0},{64,32},{96,64},{33,1},{65,33},{97,65},{34,2},{66,34},{98,6... | collective-permute-start | bytes 3145736 | tf_op jit(solution)/shard_map/ppermute | solution.py:14
  119.2 2.6 copy-start.42
  119.2 2.7 copy-start.3
  121.9 4.2 copy-start.25
  135.0 21.4 %all-to-all-start.2 = ((bf16[32,32,512]{2,1,0:T(8,128)(2,1)}), bf16[32,32,512]{2,1,0:T(8,128)(2,1)}, u32[]{:S(2)}, u32[]{:S(2)}) async-start(bf16[32,32,512]{2,1,0:T(8,128)(2,1)} %bitcast.125), calls=%async_computation.2 | async-start | bytes 2097152 | tf_op jit(solution)/shard_map/all_to_all | solution.py:87
  156.5 3.0 copy-start.11
  156.5 3.0 copy-start.14
  156.5 3.2 copy-start.29
  156.5 3.4 copy-start.40
  159.9 28.4 %copy-start.8 = (f32[1024,512]{1,0:T(8,128)S(1)}, f32[1024,512]{1,0:T(8,128)}, u32[]{:S(2)}) copy-start(f32[1024,512]{1,0:T(8,128)} %copy-done.6) | copy-start | bytes 6291460
  160.9 27.3 %collective-permute-start.1 = (bf16[1024,512]{1,0:T(8,128)(2,1)S(1)}, bf16[1024,512]{1,0:T(8,128)(2,1)S(1)}, u32[]{:S(2)}, u32[]{:S(2)}) collective-permute-start(bf16[1024,512]{1,0:T(8,128)(2,1)S(1)} %add_convert_fusion.2), channel_id=1, source_target_pairs={{32,0},{64,32},{96,64},{33,1},{65,33},{97,65},{34,2},{66,34},{98,6... | collective-permute-start | bytes 3145736 | tf_op jit(solution)/shard_map/ppermute | solution.py:14
  189.2 2.4 copy-start.41
  189.2 2.4 copy-start.4
  191.7 4.2 copy-start.26
  204.8 21.4 %all-to-all-start.3 = ((bf16[32,32,512]{2,1,0:T(8,128)(2,1)}), bf16[32,32,512]{2,1,0:T(8,128)(2,1)}, u32[]{:S(2)}, u32[]{:S(2)}) async-start(bf16[32,32,512]{2,1,0:T(8,128)(2,1)} %bitcast.124), calls=%async_computation.3 | async-start | bytes 2097152 | tf_op jit(solution)/shard_map/all_to_all | solution.py:87
  209.5 167.0 %reduce-scatter.2.cloned.1.call-start = ((), (), s32[]{:S(2)}) async-start(), calls=%async_computation.6 | async-start | bytes 7569408 | tf_op jit(solution)/shard_map/reduce_scatter | solution.py:116
  226.2 3.0 copy-start.12
  226.2 3.0 copy-start.15
  226.2 3.2 copy-start.30
  226.2 3.4 copy-start.38
  229.6 28.7 %copy-start.9 = (f32[1024,512]{1,0:T(8,128)S(1)}, f32[1024,512]{1,0:T(8,128)}, u32[]{:S(2)}) copy-start(f32[1024,512]{1,0:T(8,128)} %copy-done.6) | copy-start | bytes 6291460
  230.7 28.8 %copy-start.19 = (f32[1024,512]{0,1:T(8,128)S(1)}, f32[1024,512]{0,1:T(8,128)}, u32[]{:S(2)}) copy-start(f32[1024,512]{0,1:T(8,128)} %copy-done.18) | copy-start | bytes 6291460
  230.7 28.8 %copy-start.21 = (f32[1024,512]{0,1:T(8,128)S(1)}, f32[1024,512]{0,1:T(8,128)}, u32[]{:S(2)}) copy-start(f32[1024,512]{0,1:T(8,128)} %copy-done.20) | copy-start | bytes 6291460
  230.7 28.8 %copy-start.23 = (f32[1024,512]{0,1:T(8,128)S(1)}, f32[1024,512]{0,1:T(8,128)}, u32[]{:S(2)}) copy-start(f32[1024,512]{0,1:T(8,128)} %copy-done.22) | copy-start | bytes 6291460
  230.7 28.8 %copy-start.32 = (f32[1024,512]{0,1:T(8,128)S(1)}, f32[1024,512]{0,1:T(8,128)}, u32[]{:S(2)}) copy-start(f32[1024,512]{0,1:T(8,128)} %get-tuple-element.48) | copy-start | bytes 6291460
  230.7 27.6 %collective-permute-start.2 = (bf16[1024,512]{1,0:T(8,128)(2,1)S(1)}, bf16[1024,512]{1,0:T(8,128)(2,1)S(1)}, u32[]{:S(2)}, u32[]{:S(2)}) collective-permute-start(bf16[1024,512]{1,0:T(8,128)(2,1)S(1)} %add_convert_fusion), channel_id=1, source_target_pairs={{32,0},{64,32},{96,64},{33,1},{65,33},{97,65},{34,2},{66,34},{98,6... | collective-permute-start | bytes 3145736 | tf_op jit(solution)/shard_map/ppermute | solution.py:14
  258.3 1.1 copy-start.34
  259.5 12.1 %copy-start.27 = (bf16[1024,512]{1,0:T(8,128)(2,1)}, bf16[1024,512]{1,0:T(8,128)(2,1)S(1)}, u32[]{:S(2)}) copy-start(bf16[1024,512]{1,0:T(8,128)(2,1)S(1)} %get-tuple-element.36) | copy-start | bytes 3145732
  259.5 14.9 %copy-start.36 = (bf16[1024,512]{1,0:T(8,128)(2,1)}, bf16[1024,512]{1,0:T(8,128)(2,1)S(1)}, u32[]{:S(2)}) copy-start(bf16[1024,512]{1,0:T(8,128)(2,1)S(1)} %get-tuple-element.33) | copy-start | bytes 3145732
  259.5 3.8 copy-start.5
  269.9 1.8 copy-start.52
  276.9 1.3 copy-start.16
  279.7 3.4 copy-start.44
  280.8 3.5 copy-start.43
  283.2 2.2 copy-start.46
  284.2 2.2 copy-start.47
  285.4 2.1 copy-start.17
  285.4 2.1 copy-start.45
  294.2 5.1 %copy-start.28 = (bf16[1024,512]{1,0:T(8,128)(2,1)S(1)}, bf16[1024,512]{1,0:T(8,128)(2,1)}, u32[]{:S(2)}) copy-start(bf16[1024,512]{1,0:T(8,128)(2,1)} %copy-done.27) | copy-start | bytes 3145732
  294.2 21.8 %all-to-all-start.4 = ((bf16[32,32,512]{2,1,0:T(8,128)(2,1)}), bf16[32,32,512]{2,1,0:T(8,128)(2,1)}, u32[]{:S(2)}, u32[]{:S(2)}) async-start(bf16[32,32,512]{2,1,0:T(8,128)(2,1)} %bitcast.127), calls=%async_computation.4 | async-start | bytes 2097152 | tf_op jit(solution)/shard_map/all_to_all | solution.py:87
  299.3 119.9 %all-reduce.3.cloned.1.call-start = ((), (), s32[]{:S(2)}) async-start(), calls=%async_computation.7 | async-start | bytes 458752 | tf_op jit(solution)/shard_map/psum | solution.py:117
  316.1 60.4 %copy-start.35 = (bf16[1024,512]{1,0:T(8,128)(2,1)S(1)}, bf16[1024,512]{1,0:T(8,128)(2,1)}, u32[]{:S(2)}) copy-start(bf16[1024,512]{1,0:T(8,128)(2,1)} %copy-done.34) | copy-start | bytes 3145732
  (3 other events, 2.8 us)
Sparse Core Ops, SparseCore 0:
  290.2 86.2 reduce-scatter.1
  378.9 40.2 all-reduce.2

commit v2 on v1

--- a/solution.py
+++ b/solution.py
@@ -1,17 +1,16 @@
 import jax
 import jax.numpy as jnp
 from jax import lax
+from jax.experimental import pallas as pl
+from jax.experimental.pallas import tpu as pltpu
 from jax.sharding import PartitionSpec as P
 
 TILE = 128
+MESH = pl.DeviceIdType.MESH
+CHUNKS = 2
+BLOCK = 256
 LAST = (((1,), (1,)), ((), ()))
 FIRST = (((0,), (0,)), ((), ()))
-
-
-def shifted(block, axis, distance):
-    devices = range(lax.axis_size(axis))
-    route = [(i - distance, i) for i in devices if i - distance in devices]
-    return lax.ppermute(block, axis, route)
 
 
 def dot(a, b, dims=(((1,), (0,)), ((), ()))):
@@ -26,6 +25,174 @@
     high = value.astype(jnp.bfloat16)
     low = (value - high.astype(jnp.float32)).astype(jnp.bfloat16)
     return dot(hot, high, FIRST) + dot(hot, low, FIRST)
+
+
+def chain_kernel(
+    cot, row_factor, gate_factor, keep, target, source_t, exported_t, edge_coef,
+    basis_t, self_t, gate_t,
+    state_grad, row_grad, gate_row, edge_grad, input_grad,
+    handed, sending, total, slot_send, slot_recv,
+    z_send_sem, z_recv_sem, a_send_sem, a_recv_sem,
+):
+    bf16, f32 = jnp.bfloat16, jnp.float32
+    t, me = lax.axis_index("tm"), lax.axis_index("ent")
+    sections, ents = lax.axis_size("tm"), lax.axis_size("ent")
+    rows, width = cot.shape
+    edges, slots = target.shape[0], source_t.shape[0]
+    share = slots // ents
+    part = width // CHUNKS
+    above = lax.rem(t + 1, sections)
+    below = lax.rem(t + sections - 1, sections)
+
+    barrier = pltpu.get_barrier_semaphore()
+
+    def greet(k, carry):
+        peer = lax.rem(me + k, ents)
+        pl.semaphore_signal(barrier, inc=1, device_id=(t, peer), device_id_type=MESH)
+        return carry
+
+    lax.fori_loop(1, ents, greet, 0)
+    pl.semaphore_signal(barrier, inc=1, device_id=(above, me), device_id_type=MESH)
+    pl.semaphore_signal(barrier, inc=1, device_id=(below, me), device_id_type=MESH)
+    pl.semaphore_wait(barrier, ents + 1)
+
+    def pass_down(c):
+        return pltpu.make_async_remote_copy(
+            src_ref=sending.at[c],
+            dst_ref=handed.at[c],
+            send_sem=z_send_sem.at[c],
+            recv_sem=z_recv_sem.at[c],
+            device_id=(below, me),
+            device_id_type=MESH,
+        )
+
+    def blocks(count, body):
+        def step(i, carry):
+            body(pl.ds(pl.multiple_of(i * BLOCK, BLOCK), BLOCK))
+            return carry
+
+        lax.fori_loop(0, count // BLOCK, step, 0)
+
+    for c in range(CHUNKS):
+        cols = pl.ds(c * part, part)
+
+        @pl.when(t < sections - 1)
+        def _():
+            pass_down(c).wait_recv()
+
+        @pl.when(t == sections - 1)
+        def _():
+            handed[c] = jnp.zeros((rows, part), bf16)
+
+        def elementwise(r):
+            upstream = cot[r, cols].astype(f32) + handed[c, r, :].astype(f32)
+            row_grad[r, cols] = (upstream * row_factor[r, cols]).astype(bf16)
+            gate_row[r, cols] = (upstream * gate_factor[r, cols]).astype(bf16)
+            state_grad[r, cols] = upstream * keep[r, cols]
+
+        blocks(rows, elementwise)
+
+        def through_basis(e):
+            gathered = dot(target[e, :], row_grad[:, cols])
+            edge_grad[e, cols] = gathered.astype(bf16)
+            out = 0.0
+            for b in range(edge_coef.shape[1]):
+                image_grad = (edge_coef[e, b : b + 1] * gathered).astype(bf16)
+                out = out + dot(image_grad, basis_t[b, cols, :])
+            if c > 0:
+                out = out + total[e, :]
+            if c < CHUNKS - 1:
+                total[e, :] = out
+            else:
+                input_grad[e, :] = out.astype(bf16)
+
+        blocks(edges, through_basis)
+
+    for c in range(CHUNKS):
+        cols = pl.ds(c * part, part)
+
+        def to_slots(r):
+            slot_send[c, r, :] = dot(source_t[r, :], input_grad[:, cols]).astype(bf16)
+
+        blocks(slots, to_slots)
+        mine = pl.ds(pl.multiple_of(me * share, share), share)
+        pltpu.make_async_copy(
+            slot_send.at[c, mine], slot_recv.at[c, mine], a_recv_sem.at[c]
+        ).start()
+
+        def send(k, carry):
+            peer = lax.rem(me + k, ents)
+            pltpu.make_async_remote_copy(
+                src_ref=slot_send.at[c, pl.ds(pl.multiple_of(peer * share, share), share)],
+                dst_ref=slot_recv.at[c, mine],
+                send_sem=a_send_sem.at[c],
+                recv_sem=a_recv_sem.at[c],
+                device_id=(t, peer),
+                device_id_type=MESH,
+            ).start()
+            return carry
+
+        lax.fori_loop(1, ents, send, 0)
+
+    def local_part(r):
+        state_grad[r, :] += dot(row_grad[r, :], self_t[...]) + dot(gate_row[r, :], gate_t[...])
+
+    blocks(rows, local_part)
+
+    for c in range(CHUNKS):
+        cols = pl.ds(c * part, part)
+        pltpu.make_async_copy(slot_recv.at[c], slot_recv.at[c], a_recv_sem.at[c]).wait()
+
+        def to_rows(r):
+            out = state_grad[r, cols] + dot(exported_t[r, :], slot_recv[c])
+            state_grad[r, cols] = out
+            sending[c, r, :] = out.astype(bf16)
+
+        blocks(rows, to_rows)
+
+        @pl.when(t > 0)
+        def _():
+            pass_down(c).start()
+
+    for c in range(CHUNKS):
+        rest = slot_send.at[c, pl.ds(0, slots - share)]
+        pltpu.make_async_copy(rest, rest, a_send_sem.at[c]).wait()
+
+        @pl.when(t > 0)
+        def _():
+            pass_down(c).wait_send()
+
+
+def run_chain(*operands):
+    bf16, f32 = jnp.bfloat16, jnp.float32
+    rows, width = operands[0].shape
+    edges, slots = operands[4].shape[0], operands[5].shape[0]
+    part = width // CHUNKS
+    shape = jax.ShapeDtypeStruct
+    sem = pltpu.SemaphoreType.DMA((CHUNKS,))
+    return pl.pallas_call(
+        chain_kernel,
+        out_shape=(
+            shape((rows, width), f32),
+            shape((rows, width), bf16),
+            shape((rows, width), bf16),
+            shape((edges, width), bf16),
+            shape((edges, width), bf16),
+        ),
+        in_specs=[pl.BlockSpec(memory_space=pltpu.VMEM)] * len(operands),
+        out_specs=(pl.BlockSpec(memory_space=pltpu.VMEM),) * 5,
+        scratch_shapes=[
+            pltpu.VMEM((CHUNKS, rows, part), bf16),
+            pltpu.VMEM((CHUNKS, rows, part), bf16),
+            pltpu.VMEM((edges, width), f32),
+            pltpu.VMEM((CHUNKS, slots, part), bf16),
+            pltpu.VMEM((CHUNKS, slots, part), bf16),
+            sem, sem, sem, sem,
+        ],
+        compiler_params=pltpu.CompilerParams(
+            collective_id=0, has_side_effects=True, vmem_limit_bytes=58 << 20
+        ),
+    )(*operands)
 
 
 def per_device(
@@ -34,7 +201,6 @@
 ):
     bf16, f32 = jnp.bfloat16, jnp.float32
     ent_count = lax.axis_size("ent")
-    section_count = lax.axis_size("tm")
     state = states[0]
     rows, width = state.shape
     basis_count = basis.shape[1] // width
@@ -69,37 +235,26 @@
     row_factor = gate_open * (1.0 - aggregated * aggregated) / degree[:, None]
     gate_factor = (aggregated - state.astype(f32)) * gate_open * keep
 
-    handed = jnp.zeros((rows, width), bf16)
-    for step in range(section_count):
-        upstream = cotangent[0].astype(f32) + handed.astype(f32)
-        row_grad = (upstream * row_factor).astype(bf16)
-        gate_grad = upstream * gate_factor
-        gate_row = gate_grad.astype(bf16)
-        edge_grad = dot(target, row_grad)
-        image_grad = [
-            (edge_coef[:, b : b + 1] * edge_grad).astype(bf16) for b in range(basis_count)
-        ]
-        input_grad = sum(
-            dot(image_grad[b], basis[:, b * width : (b + 1) * width], LAST)
-            for b in range(basis_count)
-        )
-        slot_grad = dot(source, input_grad.astype(bf16), FIRST).astype(bf16)
-        returned = lax.all_to_all(slot_grad, "ent", split_axis=0, concat_axis=0, tiled=True)
-        state_grad = (
-            upstream * keep
-            + dot(row_grad, self_weight, LAST)
-            + dot(gate_row, gate_weight, LAST)
-            + dot(exported, returned, FIRST)
-        )
-        if step + 1 < section_count:
-            handed = shifted(state_grad.astype(bf16), "tm", -1)
+    basis_t = jnp.stack(
+        [basis[:, b * width : (b + 1) * width].T for b in range(basis_count)], axis=0
+    )
+    state_grad, row_grad, gate_row, edge_grad, input_grad = run_chain(
+        cotangent[0], row_factor, gate_factor, keep, target,
+        (jnp.arange(slots, dtype=jnp.int32)[:, None] == edge_src[0][None, :]).astype(bf16),
+        (jnp.arange(rows, dtype=jnp.int32)[:, None] == export_rows[0][None, :]).astype(bf16),
+        edge_coef, basis_t, self_weight.T, gate_weight.T,
+    )
+    edge_grad = edge_grad.astype(f32)
+    image_grad = [
+        (edge_coef[:, b : b + 1] * edge_grad).astype(bf16) for b in range(basis_count)
+    ]
 
     coef_edge = jnp.stack(
         [jnp.sum(edge_grad * images[b], axis=1) for b in range(basis_count)], axis=1
     )
     small = jnp.concatenate(
         [
-            jnp.sum(gate_grad, axis=0).reshape(ent_count, 1, width // ent_count),
+            jnp.sum(gate_row.astype(f32), axis=0).reshape(ent_count, 1, width // ent_count),
             split_dot(relation, coef_edge).reshape(ent_count, 1, -1),
         ],
         axis=2,
@@ -107,7 +262,7 @@
     small_width = small.shape[2]
     terms = [dot(edge_input, image_grad[b], FIRST) for b in range(basis_count)]
     terms += [dot(state, row_grad, FIRST), dot(state, gate_row, FIRST)]
-    terms += [split_dot(relation, input_grad)]
+    terms += [dot(relation, input_grad, FIRST)]
     packed = jnp.concatenate(
         [term.reshape(ent_count, -1, width) for term in terms]
         + [jnp.pad(small, ((0, 0), (0, 7), (0, width - small_width)))],

time: 438 us -> 396 us (0.904)
  Pallas kernels: 0 us -> 96.5 us
  matrix products: 123 us -> 34.2 us
  waiting for transfers between devices: 237 us -> 198 us
  starting transfers between devices: 33.4 us -> 7.67 us
  local copies, waits for them, and re-layouts: 19.6 us -> 29.3 us
  other arithmetic: 3.5 us -> 12.2 us
    reduce_scatter x1, waiting for transfers between devices: 56.1 us -> 155 us  [per_device(): share = lax.psum_scatter(packed, 'ent', scatter_dimension=0, tiled=False)]
    pallas_call x0 -> x1, Pallas kernels: none -> 96.5 us  [run_chain(): pl.pallas_call(chain_kernel, out_shape=(shape((rows, width), f32), shape(...]
    dot_general x57 -> x23, matrix products: 123 us -> 34.2 us  [dot(): return lax.dot_general(a, b, dims, preferred_element_type=jnp.float32)]
    ppermute x3 -> x0, waiting for transfers between devices: 75.4 us -> none  [shifted(): return lax.ppermute(block, axis, route)]
    all_to_all x4 -> x0, waiting for transfers between devices: 54.7 us -> none  [per_device(): lax.all_to_all(slot_grad, 'ent', split_axis=0, concat_axis=0, tiled=True)]
    all_to_all x4 -> x0, starting transfers between devices: 19 us -> none  [per_device(): lax.all_to_all(slot_grad, 'ent', split_axis=0, concat_axis=0, tiled=True)]
    all_to_all x1, waiting for transfers between devices: 14 us -> 0.01 us  [per_device(): lax.all_to_all(dot(exported, state).astype(bf16), 'ent', split_axis=0, co...]
    unnamed x121 -> x69, local copies, waits for them, and re-layouts: 13.5 us -> 22.2 us
  transfers between devices with their start and end apart: 10 -> 3, of which waited for: 10 -> 2; matrix products, arithmetic and copies ran while one was open for 7% -> 6% of each run, Pallas kernels for 0% -> 0%
where the time goes in v2:
time: 396 us; the launch traced here: 393 us
  waiting for transfers between devices  198 us (50%)
  Pallas kernels  96.5 us (24%)
  matrix products  34.2 us (9%)
  local copies, waits for them, and re-layouts  29.3 us (7%)
  between operations  15 us (4%)
  other arithmetic  12.2 us (3%)
  starting transfers between devices  7.67 us (2%)
    reduce_scatter x1, waiting for transfers between devices, per_device(): share = lax.psum_scatter(packed, 'ent', scatter_dimension=0, tiled=False)  155 us
    pallas_call x1, Pallas kernels, run_chain(): pl.pallas_call(chain_kernel, out_shape=(shape((rows, width), f32), shape(...  96.5 us
    psum x1, waiting for transfers between devices, per_device(): share = lax.psum(share, 'tm')  42.7 us
    dot_general x23, matrix products, dot(): return lax.dot_general(a, b, dims, preferred_element_type=jnp.float32)  34.2 us
    unnamed x69, local copies, waits for them, and re-layouts  22.2 us
  transfers between devices with their start and end apart: 3, of which 2 were waited for; matrix products, arithmetic and copies ran while one was open for 6% of the time, Pallas kernels for 0%

profile of v2, /device:TPU:64, one launch (start us, length us, event | category | flops | bytes accessed | tf_op | source)
XLA Modules:
  0.0 393.1 jit_solution(10598142890889190864)
XLA Ops:
  7.2 3.6 fusion.24
  10.7 7.6 %all-to-all-start = ((bf16[32,32,512]{2,1,0:T(8,128)(2,1)}), bf16[32,32,512]{2,1,0:T(8,128)(2,1)}, u32[]{:S(2)}, u32[]{:S(2)}) async-start(bf16[32,32,512]{2,1,0:T(8,128)(2,1)} %bitcast.7), calls=%async_computation | async-start | bytes 2097152 | tf_op jit(solution)/shard_map/all_to_all | solution.py:216
  19.1 0.9 convert_reduce_fusion
  20.0 0.4 fusion.46
  20.4 0.4 convolution_add_fusion.1
  20.7 0.4 convolution_add_fusion.edge_coef
  21.1 1.0 slice_reduce_fusion.3
  22.2 1.0 copy.49
  23.2 2.0 copy.50
  25.2 1.2 fusion.75
  26.5 1.3 copy.65
  27.7 2.1 copy.67
  29.8 2.1 copy.66
  31.8 1.0 copy.68
  32.8 2.9 pad_maximum_fusion.basis_t
  35.8 2.3 fusion.9.exported_t
  38.1 2.2 fusion.8.source_t
  40.3 2.0 fusion.1.target
  42.3 2.5 fusion.6
  44.8 0.5 add_convert_fusion
  45.3 0.7 fusion.69
  46.0 0.9 copy-done.6
  46.9 0.7 fusion.71
  47.6 0.7 fusion.73
  48.3 2.4 multiply_add_fusion
  50.7 1.7 fusion.2
  52.4 1.7 fusion.4
  54.2 0.9 divide_tanh_fusion
  55.0 0.1 copy-done.17
  55.2 4.0 %multiply_multiply_fusion = (f32[1024,512]{1,0:T(8,128)}, f32[1024,512]{1,0:T(8,128)}, f32[1024,512]{1,0:T(8,128)}) fusion(f32[1024,512]{1,0:T(8,128)S(1)} %divide_tanh_fusion, bf16[1,1024,512]{2,1,0:T(8,128)(2,1)S(1)} %copy-done.23, f32[1024]{0:T(1024)S(1)} %broadcast_add_fusion, f32[512]{0:T(512)S(1)} %copy-done.26, bf16[512,512]{1,0:T(8,128)(2,1)S(1)} %copy-done.17), kind=kOutput, calls=%fused_computation.32 | convolution fusion | flops 543686656 | bytes 9967616 | tf_op jit(solution)/shard_map/dot_general | solution.py:17
  59.2 96.5 %shard_map.180 = (f32[1024,512]{1,0:T(8,128)}, bf16[1024,512]{1,0:T(8,128)(2,1)}, bf16[1024,512]{1,0:T(8,128)(2,1)}, bf16[1024,512]{1,0:T(8,128)(2,1)}, bf16[1024,512]{1,0:T(8,128)(2,1)}) custom-call(bf16[1024,512]{1,0:T(8,128)(2,1)} %bitcast.82, f32[1024,512]{1,0:T(8,128)} %get-tuple-element.40.row_factor, f32[1024,512]{1,0:T(8,128)} %get-tuple-element.39.gate_factor, ...), custom_call_target="tpu_custom_call" | custom-call | tf_op jit(solution)/shard_map/pallas_call | solution.py:173
  155.8 3.1 fusion.30
  158.9 1.8 fusion.28
  160.7 1.8 fusion.26
  162.4 1.8 fusion.32
  164.2 0.8 fusion.34
  165.0 0.8 copy-done.4
  165.8 0.6 copy-done.7
  166.5 1.1 fusion.14
  167.6 0.3 fusion.45
  167.9 0.4 convolution_add_fusion.2
  168.3 0.1 reshape.72
  168.4 0.1 copy.55
  168.5 0.1 reshape.73
  168.6 2.4 fusion.36
  171.0 1.1 constant_dynamic-update-slice_fusion.5
  172.2 0.4 copy-done.13
  172.6 1.1 constant_dynamic-update-slice_fusion.4
  173.7 1.1 constant_dynamic-update-slice_fusion.3
  174.8 1.1 constant_dynamic-update-slice_fusion.2
  175.9 1.1 constant_dynamic-update-slice_fusion.1
  177.0 1.1 constant_dynamic-update-slice_fusion
  178.2 1.5 fusion.25
  179.7 0.9 pad_dynamic-update-slice_fusion
  180.6 155.4 %reduce-scatter.2.cloned.1.call-done = f32[1,112,512]{2,1,0:T(8,128)} async-done(((f32[32,112,512]{2,1,0:T(8,128)}), f32[1,112,512]{2,1,0:T(8,128)}) %reduce-scatter.2.cloned.1.call-update) | async-done | bytes 229392 | tf_op jit(solution)/shard_map/reduce_scatter | solution.py:271
  336.0 42.7 %all-reduce.3.cloned.1.call-done = f32[112,512]{1,0:T(8,128)} async-done(((f32[112,512]{1,0:T(8,128)}), f32[112,512]{1,0:T(8,128)}) %all-reduce.3.cloned.1.call-update) | async-done | bytes 229392 | tf_op jit(solution)/shard_map/psum | solution.py:272
  378.7 0.8 slice_reduce_fusion.4
  379.5 0.1 reshape_squeeze.3
  379.6 0.7 copy.57
  380.2 1.5 fusion.76
  381.7 0.7 pad_maximum_fusion.1
  382.4 1.2 slice_bitcast_fusion
  383.6 1.3 slice.88
  384.9 1.3 copy.80
  (57 shorter events, 0.3 us)
Async XLA Ops:
  7.2 37.6 %copy-start = (bf16[256,512]{1,0:T(8,128)(2,1)S(1)}, bf16[256,512]{1,0:T(8,128)(2,1)}, u32[]{:S(2)}) copy-start(bf16[256,512]{1,0:T(8,128)(2,1)} %param.22) | copy-start | bytes 786436
  10.7 8.3 %copy-start.22 = (s32[1,1024]{1,0:T(1,128)S(1)}, s32[1,1024]{1,0:T(1,128)}, u32[]{:S(2)}) copy-start(s32[1,1024]{1,0:T(1,128)} %param.17) | copy-start | bytes 12292
  10.7 9.3 %copy-start.18 = (s32[1,1024]{1,0:T(1,128)S(1)}, s32[1,1024]{1,0:T(1,128)}, u32[]{:S(2)}) copy-start(s32[1,1024]{1,0:T(1,128)} %param.18) | copy-start | bytes 12292
  10.7 9.3 %copy-start.19 = (f32[256,4]{0,1:T(4,128)S(1)}, f32[256,4]{0,1:T(4,128)}, u32[]{:S(2)}) copy-start(f32[256,4]{0,1:T(4,128)} %param.21) | copy-start | bytes 12292
  10.7 31.5 %all-to-all-start = ((bf16[32,32,512]{2,1,0:T(8,128)(2,1)}), bf16[32,32,512]{2,1,0:T(8,128)(2,1)}, u32[]{:S(2)}, u32[]{:S(2)}) async-start(bf16[32,32,512]{2,1,0:T(8,128)(2,1)} %bitcast.7), calls=%async_computation | async-start | bytes 2097152 | tf_op jit(solution)/shard_map/all_to_all | solution.py:216
  18.3 317.7 %reduce-scatter.2.cloned.1.call-start = ((), (), s32[]{:S(2)}) async-start(), calls=%async_computation.2 | async-start | bytes 7569408 | tf_op jit(solution)/shard_map/reduce_scatter | solution.py:271
  20.4 1.8 copy-start.15
  21.1 4.1 %copy-start.2 = (f32[1024,4]{1,0:T(8,128)}, f32[1024,4]{1,0:T(8,128)S(1)}, u32[]{:S(2)}) copy-start(f32[1024,4]{1,0:T(8,128)S(1)} %convolution_add_fusion.edge_coef) | copy-start | bytes 49156
  21.1 4.1 %copy-start.5 = (bf16[512,2048]{1,0:T(8,128)(2,1)S(1)}, bf16[512,2048]{1,0:T(8,128)(2,1)}, u32[]{:S(2)}) copy-start(bf16[512,2048]{1,0:T(8,128)(2,1)} %param.20) | copy-start | bytes 6291460
  32.8 2.9 copy-start.20
  35.8 2.3 copy-start.21
  45.3 1.6 copy-start.6
  48.3 2.4 copy-start.3
  52.4 1.7 copy-start.16
  52.4 1.7 copy-start.23
  54.1 1.0 copy-start.17
  54.2 1.0 copy-start.26
  155.8 3.1 copy-start.10
  162.4 1.8 copy-start.9
  162.4 1.8 copy-start.24
  164.2 1.6 copy-start.4
  164.2 2.2 copy-start.7
  168.6 2.4 copy-start.14
  171.0 1.6 copy-start.13
  171.0 2.7 copy-start.12
  172.6 2.2 copy-start.11
  175.9 2.2 copy-start.25
  180.6 204.3 %copy-start.8 = (f32[1024,512]{1,0:T(8,128)S(1)}, f32[1024,512]{1,0:T(8,128)}, u32[]{:S(2)}) copy-start(f32[1024,512]{1,0:T(8,128)} %get-tuple-element.12) | copy-start | bytes 6291460
  180.6 198.1 %all-reduce.3.cloned.1.call-start = ((), (), s32[]{:S(2)}) async-start(), calls=%async_computation.3 | async-start | bytes 458752 | tf_op jit(solution)/shard_map/psum | solution.py:272
  384.9 1.3 copy-start.1
Sparse Core Ops, SparseCore 0:
  180.7 155.2 reduce-scatter.1
  338.4 40.2 all-reduce.2

commit v3 on v2

--- a/solution.py
+++ b/solution.py
@@ -9,6 +9,8 @@
 MESH = pl.DeviceIdType.MESH
 CHUNKS = 2
 BLOCK = 256
+SIDE = 4
+GROUP = 16
 LAST = (((1,), (1,)), ((), ()))
 FIRST = (((0,), (0,)), ((), ()))
 
@@ -29,10 +31,14 @@
 
 def chain_kernel(
     cot, row_factor, gate_factor, keep, target, source_t, exported_t, edge_coef,
-    basis_t, self_t, gate_t,
-    state_grad, row_grad, gate_row, edge_grad, input_grad,
+    basis_t, self_t, gate_t, images_hbm, input_t_hbm, state_t_hbm, relation_t_hbm,
+    state_grad, basis_out, self_out, gate_out, rel_out, coef_out, bias_out,
+    row_grad, gate_row, edge_grad, input_grad,
     handed, sending, total, slot_send, slot_recv,
-    z_send_sem, z_recv_sem, a_send_sem, a_recv_sem,
+    images, input_t, state_t, relation_t, scaled, coef_hi, coef_lo, small,
+    packed, pair_recv, paired, first_recv, first_sum, second_recv, shares,
+    z_send_sem, z_recv_sem, a_send_sem, a_recv_sem, load_sem,
+    pair_sem, first_send_sem, first_recv_sem, second_send_sem, second_recv_sem, share_sem,
 ):
     bf16, f32 = jnp.bfloat16, jnp.float32
     t, me = lax.axis_index("tm"), lax.axis_index("ent")
@@ -54,7 +60,22 @@
     lax.fori_loop(1, ents, greet, 0)
     pl.semaphore_signal(barrier, inc=1, device_id=(above, me), device_id_type=MESH)
     pl.semaphore_signal(barrier, inc=1, device_id=(below, me), device_id_type=MESH)
-    pl.semaphore_wait(barrier, ents + 1)
+    opposite = lax.rem(t + 2, sections)
+    pl.semaphore_signal(barrier, inc=1, device_id=(opposite, me), device_id_type=MESH)
+    loads = [
+        pltpu.make_async_copy(src, dst, load_sem.at[i])
+        for i, (src, dst) in enumerate(
+            [
+                (images_hbm, images),
+                (input_t_hbm, input_t),
+                (state_t_hbm, state_t),
+                (relation_t_hbm, relation_t),
+            ]
+        )
+    ]
+    for load in loads:
+        load.start()
+    pl.semaphore_wait(barrier, ents + 2)
 
     def pass_down(c):
         return pltpu.make_async_remote_copy(
@@ -154,6 +175,178 @@
         def _():
             pass_down(c).start()
 
+    for load in loads:
+        load.wait()
+    core = lax.rem(me, 2)
+    y = lax.rem(me // 2, SIDE)
+    x = me // (2 * SIDE)
+    sibling = me + 1 - 2 * core
+    half = width // 2
+
+    def to_pair(offset):
+        piece = pl.ds(offset, GROUP)
+        return pltpu.make_async_remote_copy(
+            src_ref=packed.at[1 - core, :, :, piece, :],
+            dst_ref=pair_recv.at[:, :, piece, :],
+            send_sem=pair_sem.at[0],
+            recv_sem=pair_sem.at[1],
+            device_id=(t, sibling),
+            device_id_type=MESH,
+        )
+
+    def pack(offset, i, value):
+        value = value.astype(bf16).reshape(SIDE, 2, GROUP, width)
+        rows_at = pl.ds(offset, GROUP)
+        for core_to in range(2):
+            for y_to in range(SIDE):
+                one = value[y_to, core_to]
+                packed[core_to, 0, i * SIDE + y_to, rows_at, :] = one[:, :half]
+                packed[core_to, 1, y_to * SIDE + i, rows_at, :] = one[:, half:]
+
+    def term(offset, left, right):
+        def step(i, carry):
+            r = pl.ds(pl.multiple_of(i * 128, 128), 128)
+            pack(offset, i, dot(left[r, :], right[...]))
+            return carry
+
+        lax.fori_loop(0, SIDE, step, 0)
+        to_pair(offset).start()
+
+    basis_count = edge_coef.shape[1]
+    for b in range(basis_count):
+
+        def scale(e):
+            scaled[e, :] = (edge_coef[e, b : b + 1] * edge_grad[e, :].astype(f32)).astype(bf16)
+
+        blocks(edges, scale)
+        term(b * GROUP, input_t, scaled)
+    term(basis_count * GROUP, state_t, row_grad)
+    term((basis_count + 1) * GROUP, state_t, gate_row)
+
+    def inner(e):
+        lane = lax.broadcasted_iota(jnp.int32, (BLOCK, 128), 1)
+        out = jnp.zeros((BLOCK, 128), f32)
+        gradient = edge_grad[e, :].astype(f32)
+        for b in range(basis_count):
+            product = gradient * images[e, b * width : (b + 1) * width].astype(f32)
+            out = jnp.where(lane == b, jnp.sum(product, axis=1, keepdims=True), out)
+        high = out.astype(bf16)
+        coef_hi[e, :] = high
+        coef_lo[e, :] = (out - high.astype(f32)).astype(bf16)
+
+    blocks(edges, inner)
+    relations = relation_t.shape[0]
+    bias = jnp.zeros((1, width), f32)
+    for i in range(rows // BLOCK):
+        piece = gate_row[i * BLOCK : (i + 1) * BLOCK, :].astype(f32)
+        bias = bias + jnp.sum(piece, axis=0, keepdims=True)
+    line = lax.broadcasted_iota(jnp.int32, (8, width - 128), 0)
+    wrapped = jnp.concatenate([bias[:, width - 128 :]] * (width // 128 - 1), axis=1)
+    tile = jnp.where(line == 0, bias[:, : width - 128], jnp.where(line == 1, wrapped, 0.0))
+    small[:, 0:8, :] = dot(relation_t[...], input_grad[...]).reshape(ents, 8, width)
+    coef_rows = dot(relation_t[...], coef_hi[...]) + dot(relation_t[...], coef_lo[...])
+    small[:, 8:16, 0:128] = coef_rows.reshape(ents, 8, 128)
+    small[:, 8:16, 128:] = jnp.broadcast_to(tile[None], (ents, 8, width - 128))
+
+    def pack_small(i, carry):
+        pack((basis_count + 2) * GROUP, i, small[pl.ds(i * 2 * SIDE, 2 * SIDE)])
+        return carry
+
+    lax.fori_loop(0, SIDE, pack_small, 0)
+    to_pair((basis_count + 2) * GROUP).start()
+
+    pltpu.make_async_copy(pair_recv, pair_recv, pair_sem.at[1]).wait()
+
+    def chip(px, py):
+        return (t, px * (2 * SIDE) + py * 2 + core)
+
+    def other(h, k):
+        return lax.rem((x if h == 0 else y) + k, SIDE)
+
+    for h in range(2):
+
+        def add_pair(i, carry):
+            total_pair = packed[core, h, i].astype(f32) + pair_recv[h, i].astype(f32)
+            paired[h, i] = total_pair.astype(bf16)
+            return carry
+
+        lax.fori_loop(0, SIDE * SIDE, add_pair, 0)
+        for k in range(1, SIDE):
+            to = other(h, k)
+            pltpu.make_async_remote_copy(
+                src_ref=paired.at[h, pl.ds(to * SIDE, SIDE)],
+                dst_ref=first_recv.at[h, k - 1],
+                send_sem=first_send_sem.at[h],
+                recv_sem=first_recv_sem.at[h],
+                device_id=chip(to, y) if h == 0 else chip(x, to),
+                device_id_type=MESH,
+            ).start()
+
+    for h in range(2):
+        pltpu.make_async_copy(first_recv.at[h], first_recv.at[h], first_recv_sem.at[h]).wait()
+
+        def add_first(j, carry):
+            out = paired[h, other(h, 0) * SIDE + j].astype(f32)
+            for k in range(SIDE - 1):
+                out = out + first_recv[h, k, j].astype(f32)
+            first_sum[h, j] = out.astype(bf16)
+            return carry
+
+        lax.fori_loop(0, SIDE, add_first, 0)
+        for k in range(1, SIDE):
+            to = other(1 - h, k)
+            pltpu.make_async_remote_copy(
+                src_ref=first_sum.at[h, to],
+                dst_ref=second_recv.at[h, k - 1],
+                send_sem=second_send_sem.at[h],
+                recv_sem=second_recv_sem.at[h],
+                device_id=chip(x, to) if h == 0 else chip(to, y),
+                device_id_type=MESH,
+            ).start()
+
+    for h in range(2):
+        pltpu.make_async_copy(second_recv.at[h], second_recv.at[h], second_recv_sem.at[h]).wait()
+        out = first_sum[h, other(1 - h, 0)].astype(f32)
+        for k in range(SIDE - 1):
+            out = out + second_recv[h, k].astype(f32)
+        shares[t, h] = out.astype(bf16)
+    for k in range(1, SIDE):
+        pltpu.make_async_remote_copy(
+            src_ref=shares.at[t],
+            dst_ref=shares.at[t],
+            send_sem=share_sem.at[0],
+            recv_sem=share_sem.at[1],
+            device_id=(lax.rem(t + k, sections), me),
+            device_id_type=MESH,
+        ).start()
+    others = shares.at[pl.ds(0, sections - 1)]
+    pltpu.make_async_copy(others, others, share_sem.at[1]).wait()
+    for h in range(2):
+        at = pl.ds(h * half, half)
+        out = shares[0, h].astype(f32)
+        for p in range(1, SIDE):
+            out = out + shares[p, h].astype(f32)
+        for b in range(basis_count):
+            basis_out[:, b * width + h * half : b * width + (h + 1) * half] = out[
+                b * GROUP : (b + 1) * GROUP
+            ]
+        top = basis_count * GROUP
+        self_out[:, at] = out[top : top + GROUP]
+        gate_out[:, at] = out[top + GROUP : top + 2 * GROUP]
+        rel_out[:, at] = out[top + 2 * GROUP : top + 2 * GROUP + 8]
+        rest = out[top + 2 * GROUP + 8 : top + 3 * GROUP]
+        if h == 0:
+            coef_out[...] = rest[:, :128]
+            bias_out[:, : half - 128] = rest[:, 128:]
+        else:
+            bias_out[:, half - 128 :] = rest
+
+    pltpu.make_async_copy(pair_recv, pair_recv, pair_sem.at[0]).wait()
+    pltpu.make_async_copy(others, others, share_sem.at[0]).wait()
+    for h in range(2):
+        pltpu.make_async_copy(first_recv.at[h], first_recv.at[h], first_send_sem.at[h]).wait()
+        pltpu.make_async_copy(second_recv.at[h], second_recv.at[h], second_send_sem.at[h]).wait()
+
     for c in range(CHUNKS):
         rest = slot_send.at[c, pl.ds(0, slots - share)]
         pltpu.make_async_copy(rest, rest, a_send_sem.at[c]).wait()
@@ -167,30 +360,59 @@
     bf16, f32 = jnp.bfloat16, jnp.float32
     rows, width = operands[0].shape
     edges, slots = operands[4].shape[0], operands[5].shape[0]
-    part = width // CHUNKS
+    basis_count = operands[7].shape[1]
+    relations = operands[14].shape[0]
+    ents = lax.axis_size("ent")
+    part, half = width // CHUNKS, width // 2
+    height = (basis_count + 3) * GROUP
     shape = jax.ShapeDtypeStruct
-    sem = pltpu.SemaphoreType.DMA((CHUNKS,))
+    chunk_sem = pltpu.SemaphoreType.DMA((CHUNKS,))
+    two = pltpu.SemaphoreType.DMA((2,))
+    whole = pl.BlockSpec(memory_space=pltpu.VMEM)
     return pl.pallas_call(
         chain_kernel,
         out_shape=(
             shape((rows, width), f32),
-            shape((rows, width), bf16),
-            shape((rows, width), bf16),
-            shape((edges, width), bf16),
-            shape((edges, width), bf16),
+            shape((GROUP, basis_count * width), f32),
+            shape((GROUP, width), f32),
+            shape((GROUP, width), f32),
+            shape((8, width), f32),
+            shape((8, 128), f32),
+            shape((8, width - 128), f32),
         ),
-        in_specs=[pl.BlockSpec(memory_space=pltpu.VMEM)] * len(operands),
-        out_specs=(pl.BlockSpec(memory_space=pltpu.VMEM),) * 5,
+        in_specs=[whole] * 11 + [pl.BlockSpec(memory_space=pl.ANY)] * 4,
+        out_specs=(whole,) * 7,
         scratch_shapes=[
+            pltpu.VMEM((rows, width), bf16),
+            pltpu.VMEM((rows, width), bf16),
+            pltpu.VMEM((edges, width), bf16),
+            pltpu.VMEM((edges, width), bf16),
             pltpu.VMEM((CHUNKS, rows, part), bf16),
             pltpu.VMEM((CHUNKS, rows, part), bf16),
             pltpu.VMEM((edges, width), f32),
             pltpu.VMEM((CHUNKS, slots, part), bf16),
             pltpu.VMEM((CHUNKS, slots, part), bf16),
-            sem, sem, sem, sem,
+            pltpu.VMEM((edges, basis_count * width), bf16),
+            pltpu.VMEM((width, edges), bf16),
+            pltpu.VMEM((width, rows), bf16),
+            pltpu.VMEM((relations, edges), bf16),
+            pltpu.VMEM((edges, width), bf16),
+            pltpu.VMEM((edges, 128), bf16),
+            pltpu.VMEM((edges, 128), bf16),
+            pltpu.VMEM((ents, GROUP, width), f32),
+            pltpu.VMEM((2, 2, SIDE * SIDE, height, half), bf16),
+            pltpu.VMEM((2, SIDE * SIDE, height, half), bf16),
+            pltpu.VMEM((2, SIDE * SIDE, height, half), bf16),
+            pltpu.VMEM((2, SIDE - 1, SIDE, height, half), bf16),
+            pltpu.VMEM((2, SIDE, height, half), bf16),
+            pltpu.VMEM((2, SIDE - 1, height, half), bf16),
+            pltpu.VMEM((SIDE, 2, height, half), bf16),
+            chunk_sem, chunk_sem, chunk_sem, chunk_sem,
+            pltpu.SemaphoreType.DMA((4,)),
+            two, two, two, two, two, two,
         ],
         compiler_params=pltpu.CompilerParams(
-            collective_id=0, has_side_effects=True, vmem_limit_bytes=58 << 20
+            collective_id=0, has_side_effects=True, vmem_limit_bytes=60 << 20
         ),
     )(*operands)
 
@@ -238,48 +460,28 @@
     basis_t = jnp.stack(
         [basis[:, b * width : (b + 1) * width].T for b in range(basis_count)], axis=0
     )
-    state_grad, row_grad, gate_row, edge_grad, input_grad = run_chain(
+    slot_ids = jnp.arange(slots, dtype=jnp.int32)[:, None]
+    row_ids = jnp.arange(rows, dtype=jnp.int32)[:, None]
+    relation_ids = jnp.arange(relations, dtype=jnp.int32)[:, None]
+    state_grad, basis_sum, self_sum, gate_sum, rel_sum, coef_sum, bias_sum = run_chain(
         cotangent[0], row_factor, gate_factor, keep, target,
-        (jnp.arange(slots, dtype=jnp.int32)[:, None] == edge_src[0][None, :]).astype(bf16),
-        (jnp.arange(rows, dtype=jnp.int32)[:, None] == export_rows[0][None, :]).astype(bf16),
+        (slot_ids == edge_src[0][None, :]).astype(bf16),
+        (row_ids == export_rows[0][None, :]).astype(bf16),
         edge_coef, basis_t, self_weight.T, gate_weight.T,
+        jnp.concatenate([image.astype(bf16) for image in images], axis=1),
+        edge_input.T, state.T,
+        (relation_ids == edge_rel[0][None, :]).astype(bf16),
     )
-    edge_grad = edge_grad.astype(f32)
-    image_grad = [
-        (edge_coef[:, b : b + 1] * edge_grad).astype(bf16) for b in range(basis_count)
-    ]
-
-    coef_edge = jnp.stack(
-        [jnp.sum(edge_grad * images[b], axis=1) for b in range(basis_count)], axis=1
-    )
-    small = jnp.concatenate(
-        [
-            jnp.sum(gate_row.astype(f32), axis=0).reshape(ent_count, 1, width // ent_count),
-            split_dot(relation, coef_edge).reshape(ent_count, 1, -1),
-        ],
-        axis=2,
-    )
-    small_width = small.shape[2]
-    terms = [dot(edge_input, image_grad[b], FIRST) for b in range(basis_count)]
-    terms += [dot(state, row_grad, FIRST), dot(state, gate_row, FIRST)]
-    terms += [dot(relation, input_grad, FIRST)]
-    packed = jnp.concatenate(
-        [term.reshape(ent_count, -1, width) for term in terms]
-        + [jnp.pad(small, ((0, 0), (0, 7), (0, width - small_width)))],
-        axis=1,
-    )
-    share = lax.psum_scatter(packed, "ent", scatter_dimension=0, tiled=False)
-    share = lax.psum(share, "tm")
     height = width // ent_count
-    top = basis_count * height
+    bias = jnp.concatenate([bias_sum[0], bias_sum[1, :128]])
     return (
         state_grad[None],
-        jnp.concatenate([share[b * height : (b + 1) * height] for b in range(basis_count)], axis=1),
-        share[top : top + height],
-        share[top + height : top + 2 * height],
-        share[-8, :height],
-        share[-8, height:small_width].reshape(relations // ent_count, basis_count),
-        share[top + 2 * height : -8],
+        basis_sum,
+        self_sum,
+        gate_sum,
+        lax.dynamic_slice_in_dim(bias, lax.axis_index("ent") * height, height, 0),
+        coef_sum[:, :basis_count],
+        rel_sum,
     )
 
 

time: 396 us -> 287 us (0.72)
  waiting for transfers between devices: 198 us -> 0.01 us
  Pallas kernels: 96.5 us -> 202 us
  between operations: 15 us -> 1.55 us
  matrix products: 34.2 us -> 29.4 us
    reduce_scatter x1 -> x0, waiting for transfers between devices: 155 us -> none  [per_device(): share = lax.psum_scatter(packed, 'ent', scatter_dimension=0, tiled=False)]
    pallas_call x1, Pallas kernels: 96.5 us -> 202 us  [run_chain(): pl.pallas_call(chain_kernel, out_shape=(shape((rows, width), f32), shape(...]
    psum x1 -> x0, waiting for transfers between devices: 42.7 us -> none  [per_device(): share = lax.psum(share, 'tm')]
    unnamed x69 -> x66, local copies, waits for them, and re-layouts: 22.2 us -> 14 us
    dot_general x0 -> x4, local copies, waits for them, and re-layouts: none -> 7.8 us  [dot(): return lax.dot_general(a, b, dims, preferred_element_type=jnp.float32)]
    dot_general x23 -> x14, matrix products: 34.2 us -> 29.4 us  [dot(): return lax.dot_general(a, b, dims, preferred_element_type=jnp.float32)]
  transfers between devices with their start and end apart: 3 -> 1, of which waited for: 2 -> 0; matrix products, arithmetic and copies ran while one was open for 6% -> 6% of each run, Pallas kernels for 0% -> 0%
where the time goes in v3:
time: 287 us
  Pallas kernels  202 us (70%)
  local copies, waits for them, and re-layouts  32.6 us (11%)
  matrix products  29.4 us (10%)
  other arithmetic  13.2 us (5%)
  starting transfers between devices  7.59 us (3%)
    pallas_call x1, Pallas kernels, run_chain(): pl.pallas_call(chain_kernel, out_shape=(shape((rows, width), f32), shape(...  202 us
    dot_general x14, matrix products, dot(): return lax.dot_general(a, b, dims, preferred_element_type=jnp.float32)  29.4 us
    unnamed x66, local copies, waits for them, and re-layouts  14 us
    dot_general x4, local copies, waits for them, and re-layouts, dot(): return lax.dot_general(a, b, dims, preferred_element_type=jnp.float32)  7.8 us
    all_to_all x1, starting transfers between devices, per_device(): lax.all_to_all(dot(exported, state).astype(bf16), 'ent', split_axis=0, co...  7.59 us
  transfers between devices with their start and end apart: 1, of which 0 were waited for; matrix products, arithmetic and copies ran while one was open for 6% of the time, Pallas kernels for 0%

profile of v3, /device:TPU:64, one launch (start us, length us, event | category | flops | bytes accessed | tf_op | source)
XLA Modules:
  0.0 286.6 jit_solution(4637236947898855960)
XLA Ops:
  0.6 0.0 copy-start
  0.6 3.5 %fusion.16 = bf16[1024,512]{1,0:T(8,128)(2,1)} fusion(s32[1024]{0:T(1024)} %bitcast.66, bf16[1,1024,512]{2,1,0:T(8,128)(2,1)} %param.13), kind=kOutput, calls=%fused_computation.29 | convolution fusion | flops 1075314688 | bytes 2101248 | tf_op jit(solution)/shard_map/dot_general | solution.py:19
  4.2 7.6 %all-to-all-start = ((bf16[32,32,512]{2,1,0:T(8,128)(2,1)}), bf16[32,32,512]{2,1,0:T(8,128)(2,1)}, u32[]{:S(2)}, u32[]{:S(2)}) async-start(bf16[32,32,512]{2,1,0:T(8,128)(2,1)} %bitcast.7), calls=%async_computation | async-start | bytes 2097152 | tf_op jit(solution)/shard_map/all_to_all | solution.py:438
  11.8 0.0 copy-done.11
  11.8 1.3 copy.44
  13.1 0.0 copy-done.17
  13.2 0.9 fusion.21.relation_t_hbm
  14.1 0.0 copy-done.18
  14.1 0.3 fusion.20
  14.4 0.0 copy-start.24
  14.4 0.0 copy-start.4
  14.5 0.4 convolution_add_fusion.1
  14.8 0.4 convolution_add_fusion.edge_coef
  15.2 0.0 copy-start.3
  15.2 1.0 slice_reduce_fusion.3
  16.9 0.9 convert_reduce_fusion
  17.9 0.2 fusion.43
  18.0 0.0 copy-start.13
  18.0 0.2 copy.77
  18.3 0.2 copy.78
  18.5 0.2 copy.79
  18.7 0.2 copy.80
  18.9 0.2 copy-done.13
  19.1 1.0 copy.58
  20.1 2.1 copy.59
  22.2 1.6 pad_maximum_fusion.1.basis_t
  23.8 2.3 fusion.9.exported_t
  26.0 2.2 fusion.8.source_t
  28.2 2.0 fusion.1.target
  30.2 0.0 all-to-all-done
  30.2 2.7 fusion.6
  32.9 0.0 copy-start.5
  32.9 0.6 add_convert_fusion
  33.6 1.0 copy-done.5
  34.5 0.7 fusion.37
  35.2 2.1 fusion.39
  37.4 2.1 fusion.41
  39.4 2.5 copy.60
  42.0 2.5 copy.61
  44.5 1.4 copy.62
  45.9 4.4 %multiply_add_fusion = (f32[1024,512]{0,1:T(8,128)S(1)}, bf16[1024,512]{0,1:T(8,128)(2,1)}) fusion(f32[1024,512]{0,1:T(8,128)S(1)} %fusion.37, f32[1024,512]{0,1:T(8,128)} %fusion.39, f32[1024,512]{0,1:T(8,128)} %fusion.41, f32[1024]{0:T(1024)S(1)} %get-tuple-element.36, f32[1024]{0:T(1024)S(1)} %get-tuple-element.37, f32[1024]{0:T(1024)S(1)} %get-tuple-element.38, ...), kind=kOutput, calls=%fused_computation.20 | convolution fusion | flops 541065216 | bytes 11026432 | tf_op jit(solution)/shard_map/dot_general | solution.py:19
  50.3 2.9 fusion.2
  53.1 2.8 fusion.4
  55.9 1.3 copy.63
  57.3 0.4 copy-done.14
  57.7 3.1 %divide_tanh_fusion = f32[1024,512]{0,1:T(8,128)S(1)} fusion(f32[1024,512]{0,1:T(8,128)} %fusion.4, f32[1024,512]{0,1:T(8,128)} %fusion.2, bf16[512,512]{1,0:T(8,128)(2,1)S(1)} %copy-done.14, bf16[1,1024,512]{2,1,0:T(8,128)(2,1)S(1)} %copy-done.12, f32[1024]{0:T(1024)S(1)} %broadcast_add_fusion), kind=kOutput, calls=%fused_computation.18 | convolution fusion | flops 538443776 | bytes 7868416 | tf_op jit(solution)/shard_map/dot_general | solution.py:19
  60.8 3.5 %multiply_multiply_fusion = (f32[1024,512]{0,1:T(8,128)S(1)}, f32[1024,512]{0,1:T(8,128)}, f32[1024,512]{0,1:T(8,128)}) fusion(f32[1024,512]{0,1:T(8,128)S(1)} %divide_tanh_fusion, bf16[1,1024,512]{1,2,0:T(8,128)(2,1)S(1)} %copy-done.6, f32[1024]{0:T(1024)S(1)} %broadcast_add_fusion, f32[512]{0:T(512)S(1)} %copy-done.25, ...), kind=kOutput, calls=%fused_computation.16 | convolution fusion | flops 543686656 | bytes 11016192 | tf_op jit(solution)/shard_map/dot_general | solution.py:19
  64.3 2.9 %copy.64.row_factor = f32[1024,512]{1,0:T(8,128)} copy(f32[1024,512]{0,1:T(8,128)} %get-tuple-element.40) | data formatting | bytes 4194304 | tf_op jit(solution)/shard_map/div | solution.py:457
  67.2 1.8 copy.65.gate_factor
  69.0 3.0 %copy.66.keep = f32[1024,512]{1,0:T(8,128)} copy(f32[1024,512]{0,1:T(8,128)} %get-tuple-element.45) | data formatting | bytes 4194304 | tf_op jit(solution)/shard_map/sub | solution.py:456
  72.1 0.0 copy-done.7
  72.1 0.0 copy-done.9
  72.1 3.3 %pad_maximum_fusion.images_hbm = bf16[1024,2048]{1,0:T(8,128)(2,1)} fusion(bf16[1024,512]{1,0:T(8,128)(2,1)} %copy.63, bf16[1024,512]{1,0:T(8,128)(2,1)S(1)} %copy-done.9, bf16[1024,512]{1,0:T(8,128)(2,1)S(1)} %copy-done.8, bf16[1024,512]{1,0:T(8,128)(2,1)S(1)} %copy-done.7), kind=kLoop, calls=%fused_computation | loop fusion | flops 16777216 | bytes 8388608 | tf_op jit(solution)/shard_map/concatenate | solution.py:471
  75.4 202.2 %shard_map.180 = (f32[1024,512]{1,0:T(8,128)}, f32[16,2048]{1,0:T(8,128)}, f32[16,512]{1,0:T(8,128)}, f32[16,512]{1,0:T(8,128)}, f32[8,512]{1,0:T(8,128)}, /*index=5*/f32[8,128]{1,0:T(8,128)}, f32[8,384]{1,0:T(8,128)}) custom-call(bf16[1024,512]{1,0:T(8,128)(2,1)} %bitcast.60, f32[1024,512]{1,0:T(8,128)} %copy.64.row_factor, f32[1024,512]{1,0:T(8,128)} %copy.65.gate_factor, ...), custom_call_target="tpu_custom_call" | custom-call | tf_op jit(solution)/shard_map/pallas_call | solution.py:372
  277.6 0.7 slice_reduce_fusion.4
  278.3 0.7 slice_bitcast_fusion
  279.0 1.3 copy.67
  280.3 0.6 dynamic_slice.3
  280.9 3.1 %copy.87 = f32[1,1024,512]{2,1,0:T(8,128)} copy(f32[1,1024,512]{2,1,0:T(8,128)} %bitcast.55) | data formatting | bytes 4194304
  284.1 0.7 copy.88
  284.7 0.6 copy.89
  285.3 0.0 copy-done.19
  285.3 0.6 copy.90
  285.9 0.6 copy.91
  (40 shorter events, 0.1 us)
Async XLA Ops:
  0.6 32.3 %copy-start = (bf16[256,512]{1,0:T(8,128)(2,1)S(1)}, bf16[256,512]{1,0:T(8,128)(2,1)}, u32[]{:S(2)}) copy-start(bf16[256,512]{1,0:T(8,128)(2,1)} %param.22) | copy-start | bytes 786436
  4.2 7.6 %copy-start.11 = (bf16[1,1024,512]{2,1,0:T(8,128)(2,1)S(1)}, bf16[1,1024,512]{2,1,0:T(8,128)(2,1)}, u32[]{:S(2)}) copy-start(bf16[1,1024,512]{2,1,0:T(8,128)(2,1)} %param.13) | copy-start | bytes 3145732
  4.2 9.0 %copy-start.17 = (s32[1,1024]{1,0:T(1,128)S(1)}, s32[1,1024]{1,0:T(1,128)}, u32[]{:S(2)}) copy-start(s32[1,1024]{1,0:T(1,128)} %param.18) | copy-start | bytes 12292
  4.2 9.9 %copy-start.18 = (f32[256,4]{0,1:T(4,128)S(1)}, f32[256,4]{0,1:T(4,128)}, u32[]{:S(2)}) copy-start(f32[256,4]{0,1:T(4,128)} %param.21) | copy-start | bytes 12292
  4.2 26.0 %all-to-all-start = ((bf16[32,32,512]{2,1,0:T(8,128)(2,1)}), bf16[32,32,512]{2,1,0:T(8,128)(2,1)}, u32[]{:S(2)}, u32[]{:S(2)}) async-start(bf16[32,32,512]{2,1,0:T(8,128)(2,1)} %bitcast.7), calls=%async_computation | async-start | bytes 2097152 | tf_op jit(solution)/shard_map/all_to_all | solution.py:438
  14.4 2.5 copy-start.24
  14.4 3.4 %copy-start.4 = (bf16[512,2048]{1,0:T(8,128)(2,1)S(1)}, bf16[512,2048]{1,0:T(8,128)(2,1)}, u32[]{:S(2)}) copy-start(bf16[512,2048]{1,0:T(8,128)(2,1)} %param.20) | copy-start | bytes 6291460
  15.2 2.8 copy-start.3
  18.0 1.0 copy-start.13
  22.2 1.6 copy-start.22
  23.8 2.3 copy-start.23
  32.9 1.6 copy-start.5
  34.5 11.4 %copy-start.2 = (bf16[1024,512]{0,1:T(8,128)(2,1)}, bf16[1024,512]{0,1:T(8,128)(2,1)S(1)}, u32[]{:S(2)}) copy-start(bf16[1024,512]{0,1:T(8,128)(2,1)S(1)} %add_convert_fusion) | copy-start | bytes 3145732
  53.1 2.8 copy-start.10
  55.9 1.3 copy-start.12
  55.9 1.7 copy-start.14
  57.7 3.1 %copy-start.6 = (bf16[1,1024,512]{1,2,0:T(8,128)(2,1)S(1)}, bf16[1,1024,512]{1,2,0:T(8,128)(2,1)}, u32[]{:S(2)}) copy-start(bf16[1,1024,512]{1,2,0:T(8,128)(2,1)} %copy.44) | copy-start | bytes 3145732
  57.7 3.1 %copy-start.15 = (bf16[512,512]{1,0:T(8,128)(2,1)S(1)}, bf16[512,512]{1,0:T(8,128)(2,1)}, u32[]{:S(2)}) copy-start(bf16[512,512]{1,0:T(8,128)(2,1)} %param.24) | copy-start | bytes 1572868
  57.7 3.1 %copy-start.25 = (f32[512]{0:T(512)S(1)}, f32[512]{0:T(512)}, u32[]{:S(2)}) copy-start(f32[512]{0:T(512)} %param.25) | copy-start | bytes 6148
  69.0 3.1 %copy-start.7 = (bf16[1024,512]{1,0:T(8,128)(2,1)S(1)}, bf16[1024,512]{1,0:T(8,128)(2,1)}, u32[]{:S(2)}) copy-start(bf16[1024,512]{1,0:T(8,128)(2,1)} %copy.60) | copy-start | bytes 3145732
  69.0 3.1 %copy-start.8 = (bf16[1024,512]{1,0:T(8,128)(2,1)S(1)}, bf16[1024,512]{1,0:T(8,128)(2,1)}, u32[]{:S(2)}) copy-start(bf16[1024,512]{1,0:T(8,128)(2,1)} %copy.61) | copy-start | bytes 3145732
  69.0 3.1 %copy-start.9 = (bf16[1024,512]{1,0:T(8,128)(2,1)S(1)}, bf16[1024,512]{1,0:T(8,128)(2,1)}, u32[]{:S(2)}) copy-start(bf16[1024,512]{1,0:T(8,128)(2,1)} %copy.62) | copy-start | bytes 3145732
  280.3 6.2 %copy-start.1 = (bf16[256,512]{1,0:T(8,128)(2,1)S(1)}, bf16[256,512]{1,0:T(8,128)(2,1)}, u32[]{:S(2)}) copy-start(bf16[256,512]{1,0:T(8,128)(2,1)} %param.22) | copy-start | bytes 786436
  280.9 3.1 %copy-start.16 = (f32[16,2048]{1,0:T(8,128)S(1)}, f32[16,2048]{1,0:T(8,128)}, u32[]{:S(2)}) copy-start(f32[16,2048]{1,0:T(8,128)} %get-tuple-element.58) | copy-start | bytes 393220
  280.9 3.8 %copy-start.20 = (f32[16,512]{1,0:T(8,128)S(1)}, f32[16,512]{1,0:T(8,128)}, u32[]{:S(2)}) copy-start(f32[16,512]{1,0:T(8,128)} %get-tuple-element.59) | copy-start | bytes 98308
  280.9 4.4 %copy-start.19 = (f32[16,512]{1,0:T(8,128)S(1)}, f32[16,512]{1,0:T(8,128)}, u32[]{:S(2)}) copy-start(f32[16,512]{1,0:T(8,128)} %get-tuple-element.60) | copy-start | bytes 98308
  280.9 5.0 %copy-start.21 = (f32[8,512]{1,0:T(8,128)S(1)}, f32[8,512]{1,0:T(8,128)}, u32[]{:S(2)}) copy-start(f32[8,512]{1,0:T(8,128)} %get-tuple-element.63) | copy-start | bytes 49156

commit v4 on v3

--- a/solution.py
+++ b/solution.py
@@ -11,40 +11,35 @@
 BLOCK = 256
 SIDE = 4
 GROUP = 16
+EXPORT, SOURCE, TARGET, RELATION = range(4)
 LAST = (((1,), (1,)), ((), ()))
-FIRST = (((0,), (0,)), ((), ()))
 
 
 def dot(a, b, dims=(((1,), (0,)), ((), ()))):
     return lax.dot_general(a, b, dims, preferred_element_type=jnp.float32)
 
 
-def onehot(ids, count):
-    return ids[:, None] == jnp.arange(count, dtype=jnp.int32)[None, :]
-
-
-def split_dot(hot, value):
-    high = value.astype(jnp.bfloat16)
-    low = (value - high.astype(jnp.float32)).astype(jnp.bfloat16)
-    return dot(hot, high, FIRST) + dot(hot, low, FIRST)
-
-
 def chain_kernel(
-    cot, row_factor, gate_factor, keep, target, source_t, exported_t, edge_coef,
-    basis_t, self_t, gate_t, images_hbm, input_t_hbm, state_t_hbm, relation_t_hbm,
+    state, ids_row, ids_col, coef_parts, gate_bias,
+    cot_hbm, basis_hbm, rel_emb_hbm, self_hbm, gate_hbm,
     state_grad, basis_out, self_out, gate_out, rel_out, coef_out, bias_out,
+    cot, basis, rel_emb, self_weight, gate_weight,
+    row_factor, gate_factor, keep, target, source_t, early, exported_t, edge_coef,
+    export_send, export_recv, edge_input,
     row_grad, gate_row, edge_grad, input_grad,
     handed, sending, total, slot_send, slot_recv,
     images, input_t, state_t, relation_t, scaled, coef_hi, coef_lo, small,
-    packed, pair_recv, paired, first_recv, first_sum, second_recv, shares,
-    z_send_sem, z_recv_sem, a_send_sem, a_recv_sem, load_sem,
+    packed, pair_recv, first_recv, first_sum, second_recv, shares,
+    z_send_sem, z_recv_sem, a_send_sem, a_recv_sem, load_sem, export_sem,
     pair_sem, first_send_sem, first_recv_sem, second_send_sem, second_recv_sem, share_sem,
 ):
     bf16, f32 = jnp.bfloat16, jnp.float32
     t, me = lax.axis_index("tm"), lax.axis_index("ent")
     sections, ents = lax.axis_size("tm"), lax.axis_size("ent")
-    rows, width = cot.shape
-    edges, slots = target.shape[0], source_t.shape[0]
+    rows, width = state.shape
+    edges = slots = ids_row.shape[1]
+    relations = rel_emb.shape[0]
+    basis_count = basis.shape[1] // width
     share = slots // ents
     part = width // CHUNKS
     above = lax.rem(t + 1, sections)
@@ -66,16 +61,16 @@
         pltpu.make_async_copy(src, dst, load_sem.at[i])
         for i, (src, dst) in enumerate(
             [
-                (images_hbm, images),
-                (input_t_hbm, input_t),
-                (state_t_hbm, state_t),
-                (relation_t_hbm, relation_t),
+                (rel_emb_hbm, rel_emb),
+                (self_hbm, self_weight),
+                (gate_hbm, gate_weight),
+                (basis_hbm, basis),
+                (cot_hbm, cot),
             ]
         )
     ]
     for load in loads:
         load.start()
-    pl.semaphore_wait(barrier, ents + 2)
 
     def pass_down(c):
         return pltpu.make_async_remote_copy(
@@ -94,6 +89,88 @@
 
         lax.fori_loop(0, count // BLOCK, step, 0)
 
+    def one(mask):
+        return jnp.where(mask, 1.0, 0.0).astype(bf16)
+
+    def by_row(kind, r, count):
+        lane = lax.broadcasted_iota(jnp.int32, (BLOCK, count), 1)
+        return one(ids_col[r, kind : kind + 1] == lane)
+
+    def by_column(kind, r):
+        line = lax.broadcasted_iota(jnp.int32, (BLOCK, edges), 0) + r.start
+        return one(ids_row[kind : kind + 1, :] == line)
+
+    mine = pl.ds(pl.multiple_of(me * share, share), share)
+
+    def export(r):
+        export_send[r, :] = dot(by_row(EXPORT, r, rows), state[...]).astype(bf16)
+
+    blocks(slots, export)
+    pltpu.make_async_copy(export_send.at[mine], export_recv.at[mine], export_sem.at[1]).start()
+    pl.semaphore_wait(barrier, ents + 2)
+
+    def send_export(k, carry):
+        peer = lax.rem(me + k, ents)
+        pltpu.make_async_remote_copy(
+            src_ref=export_send.at[pl.ds(pl.multiple_of(peer * share, share), share)],
+            dst_ref=export_recv.at[mine],
+            send_sem=export_sem.at[0],
+            recv_sem=export_sem.at[1],
+            device_id=(t, peer),
+            device_id_type=MESH,
+        ).start()
+        return carry
+
+    lax.fori_loop(1, ents, send_export, 0)
+    for load in loads[:3]:
+        load.wait()
+
+    def by_edge(e):
+        early[e, :] = by_row(SOURCE, e, slots)
+        target[e, :] = by_row(TARGET, e, rows)
+        relation = by_row(RELATION, e, relations)
+        total[e, :] = dot(relation, rel_emb[...])
+        edge_coef[e, :] = sum(dot(relation, coef_parts[i]) for i in range(3))
+
+    blocks(edges, by_edge)
+
+    def forms(r):
+        exported_t[r, :] = by_column(TARGET, r)
+        source_t[r, :] = by_column(SOURCE, r)
+        state_grad[r, :] = dot(state[r, :], self_weight[...])
+        keep[r, :] = jax.nn.sigmoid(dot(state[r, :], gate_weight[...]) + gate_bias[...])
+
+    blocks(rows, forms)
+    loads[3].wait()
+    pltpu.make_async_copy(export_recv, export_recv, export_sem.at[1]).wait()
+
+    def forward(e):
+        value = (dot(early[e, :], export_recv[...]) + total[e, :]).astype(bf16)
+        edge_input[e, :] = value
+        message = 0.0
+        for b in range(basis_count):
+            at = slice(b * width, (b + 1) * width)
+            image = dot(value, basis[:, at])
+            images[e, at] = image.astype(bf16)
+            message = message + edge_coef[e, b : b + 1] * image
+        edge_grad[e, :] = message.astype(bf16)
+
+    blocks(edges, forward)
+
+    def factors(r):
+        hot = exported_t[r, :]
+        degree = 1.0 + dot(hot, jnp.ones((edges, 128), bf16))[:, :1]
+        scale = 1.0 / degree
+        aggregated = jnp.tanh((dot(hot, edge_grad[...]) + state_grad[r, :]) * scale)
+        gate_open = keep[r, :]
+        closed = 1.0 - gate_open
+        row_factor[r, :] = gate_open * (1.0 - aggregated * aggregated) * scale
+        gate_factor[r, :] = (aggregated - state[r, :].astype(f32)) * gate_open * closed
+        keep[r, :] = closed
+
+    blocks(rows, factors)
+    loads[4].wait()
+
     for c in range(CHUNKS):
         cols = pl.ds(c * part, part)
 
@@ -117,9 +194,10 @@
             gathered = dot(target[e, :], row_grad[:, cols])
             edge_grad[e, cols] = gathered.astype(bf16)
             out = 0.0
-            for b in range(edge_coef.shape[1]):
+            for b in range(basis_count):
                 image_grad = (edge_coef[e, b : b + 1] * gathered).astype(bf16)
-                out = out + dot(image_grad, basis_t[b, cols, :])
+                at = slice(b * width + c * part, b * width + (c + 1) * part)
+                out = out + dot(image_grad, basis[:, at], LAST)
             if c > 0:
                 out = out + total[e, :]
             if c < CHUNKS - 1:
@@ -136,7 +214,6 @@
             slot_send[c, r, :] = dot(source_t[r, :], input_grad[:, cols]).astype(bf16)
 
         blocks(slots, to_slots)
-        mine = pl.ds(pl.multiple_of(me * share, share), share)
         pltpu.make_async_copy(
             slot_send.at[c, mine], slot_recv.at[c, mine], a_recv_sem.at[c]
         ).start()
@@ -156,7 +233,10 @@
         lax.fori_loop(1, ents, send, 0)
 
     def local_part(r):
-        state_grad[r, :] += dot(row_grad[r, :], self_t[...]) + dot(gate_row[r, :], gate_t[...])
+        state_grad[r, :] += dot(row_grad[r, :], self_weight[...], LAST) + dot(
+            gate_row[r, :], gate_weight[...], LAST
+        )
+        exported_t[r, :] = by_column(EXPORT, r)
 
     blocks(rows, local_part)
 
@@ -175,8 +255,13 @@
         def _():
             pass_down(c).start()
 
-    for load in loads:
-        load.wait()
+    def turn(r):
+        input_t[:, r] = edge_input[r, :].T
+        state_t[:, r] = state[r, :].T
+
+    blocks(edges, turn)
+    relation_line = lax.broadcasted_iota(jnp.int32, (relations, edges), 0)
+    relation_t[...] = one(ids_row[RELATION : RELATION + 1, :] == relation_line)
     core = lax.rem(me, 2)
     y = lax.rem(me // 2, SIDE)
     x = me // (2 * SIDE)
@@ -212,7 +297,6 @@
         lax.fori_loop(0, SIDE, step, 0)
         to_pair(offset).start()
 
-    basis_count = edge_coef.shape[1]
     for b in range(basis_count):
 
         def scale(e):
@@ -235,7 +319,6 @@
         coef_lo[e, :] = (out - high.astype(f32)).astype(bf16)
 
     blocks(edges, inner)
-    relations = relation_t.shape[0]
     bias = jnp.zeros((1, width), f32)
     for i in range(rows // BLOCK):
         piece = gate_row[i * BLOCK : (i + 1) * BLOCK, :].astype(f32)
@@ -267,14 +350,14 @@
 
         def add_pair(i, carry):
             total_pair = packed[core, h, i].astype(f32) + pair_recv[h, i].astype(f32)
-            paired[h, i] = total_pair.astype(bf16)
+            packed[core, h, i] = total_pair.astype(bf16)
             return carry
 
         lax.fori_loop(0, SIDE * SIDE, add_pair, 0)
         for k in range(1, SIDE):
             to = other(h, k)
             pltpu.make_async_remote_copy(
-                src_ref=paired.at[h, pl.ds(to * SIDE, SIDE)],
+                src_ref=packed.at[core, h, pl.ds(to * SIDE, SIDE)],
                 dst_ref=first_recv.at[h, k - 1],
                 send_sem=first_send_sem.at[h],
                 recv_sem=first_recv_sem.at[h],
@@ -286,7 +369,7 @@
         pltpu.make_async_copy(first_recv.at[h], first_recv.at[h], first_recv_sem.at[h]).wait()
 
         def add_first(j, carry):
-            out = paired[h, other(h, 0) * SIDE + j].astype(f32)
+            out = packed[core, h, other(h, 0) * SIDE + j].astype(f32)
             for k in range(SIDE - 1):
                 out = out + first_recv[h, k, j].astype(f32)
             first_sum[h, j] = out.astype(bf16)
@@ -348,6 +431,9 @@
         pltpu.make_async_copy(second_recv.at[h], second_recv.at[h], second_send_sem.at[h]).wait()
 
     for c in range(CHUNKS):
+        if c == 0:
+            rest = export_send.at[pl.ds(0, slots - share)]
+            pltpu.make_async_copy(rest, rest, export_sem.at[0]).wait()
         rest = slot_send.at[c, pl.ds(0, slots - share)]
         pltpu.make_async_copy(rest, rest, a_send_sem.at[c]).wait()
 
@@ -359,9 +445,9 @@
 def run_chain(*operands):
     bf16, f32 = jnp.bfloat16, jnp.float32
     rows, width = operands[0].shape
-    edges, slots = operands[4].shape[0], operands[5].shape[0]
-    basis_count = operands[7].shape[1]
-    relations = operands[14].shape[0]
+    edges = slots = operands[1].shape[1]
+    basis_count = operands[6].shape[1] // width
+    relations = operands[7].shape[0]
     ents = lax.axis_size("ent")
     part, half = width // CHUNKS, width // 2
     height = (basis_count + 3) * GROUP
@@ -369,6 +455,12 @@
     chunk_sem = pltpu.SemaphoreType.DMA((CHUNKS,))
     two = pltpu.SemaphoreType.DMA((2,))
     whole = pl.BlockSpec(memory_space=pltpu.VMEM)
+    wide, flat, narrow = (
+        pltpu.VMEM((rows, width), f32),
+        pltpu.VMEM((rows, width), bf16),
+        pltpu.VMEM((edges, 128), bf16),
+    )
+    hot = pltpu.VMEM((rows, edges), bf16)
     return pl.pallas_call(
         chain_kernel,
         out_shape=(
@@ -380,39 +472,41 @@
             shape((8, 128), f32),
             shape((8, width - 128), f32),
         ),
-        in_specs=[whole] * 11 + [pl.BlockSpec(memory_space=pl.ANY)] * 4,
+        in_specs=[whole] * 5 + [pl.BlockSpec(memory_space=pl.ANY)] * 5,
         out_specs=(whole,) * 7,
         scratch_shapes=[
-            pltpu.VMEM((rows, width), bf16),
-            pltpu.VMEM((rows, width), bf16),
-            pltpu.VMEM((edges, width), bf16),
-            pltpu.VMEM((edges, width), bf16),
+            flat,
+            pltpu.VMEM((width, basis_count * width), bf16),
+            pltpu.VMEM((relations, width), bf16),
+            pltpu.VMEM((width, width), bf16),
+            pltpu.VMEM((width, width), bf16),
+            wide, wide, wide, hot, hot, hot, hot,
+            pltpu.VMEM((edges, 128), f32),
+            flat, flat, flat,
+            flat, flat, flat, flat,
             pltpu.VMEM((CHUNKS, rows, part), bf16),
             pltpu.VMEM((CHUNKS, rows, part), bf16),
-            pltpu.VMEM((edges, width), f32),
+            wide,
             pltpu.VMEM((CHUNKS, slots, part), bf16),
             pltpu.VMEM((CHUNKS, slots, part), bf16),
             pltpu.VMEM((edges, basis_count * width), bf16),
             pltpu.VMEM((width, edges), bf16),
             pltpu.VMEM((width, rows), bf16),
             pltpu.VMEM((relations, edges), bf16),
-            pltpu.VMEM((edges, width), bf16),
-            pltpu.VMEM((edges, 128), bf16),
-            pltpu.VMEM((edges, 128), bf16),
+            flat, narrow, narrow,
             pltpu.VMEM((ents, GROUP, width), f32),
             pltpu.VMEM((2, 2, SIDE * SIDE, height, half), bf16),
-            pltpu.VMEM((2, SIDE * SIDE, height, half), bf16),
             pltpu.VMEM((2, SIDE * SIDE, height, half), bf16),
             pltpu.VMEM((2, SIDE - 1, SIDE, height, half), bf16),
             pltpu.VMEM((2, SIDE, height, half), bf16),
             pltpu.VMEM((2, SIDE - 1, height, half), bf16),
             pltpu.VMEM((SIDE, 2, height, half), bf16),
             chunk_sem, chunk_sem, chunk_sem, chunk_sem,
-            pltpu.SemaphoreType.DMA((4,)),
-            two, two, two, two, two, two,
+            pltpu.SemaphoreType.DMA((5,)),
+            two, two, two, two, two, two, two,
         ],
         compiler_params=pltpu.CompilerParams(
-            collective_id=0, has_side_effects=True, vmem_limit_bytes=60 << 20
+            collective_id=0, has_side_effects=True, vmem_limit_bytes=63 << 20
         ),
     )(*operands)
 
@@ -423,54 +517,19 @@
 ):
     bf16, f32 = jnp.bfloat16, jnp.float32
     ent_count = lax.axis_size("ent")
-    state = states[0]
-    rows, width = state.shape
+    width = states.shape[2]
     basis_count = basis.shape[1] // width
-    relations = rel_emb.shape[0]
     edges = edge_src.shape[1]
-    slots = export_rows.shape[1]
     live = jnp.arange(edges, dtype=jnp.int32) // TILE < tile_count[0, 0]
-    source = onehot(edge_src[0], slots).astype(bf16)
-    target = (onehot(edge_dst[0], rows) & live[:, None]).astype(bf16)
-    exported = onehot(export_rows[0], rows).astype(bf16)
-    relation = onehot(edge_rel[0], relations).astype(bf16)
-
-    received = lax.all_to_all(
-        dot(exported, state).astype(bf16), "ent", split_axis=0, concat_axis=0, tiled=True
-    )
-    edge_input = (dot(source, received) + dot(relation, rel_emb)).astype(bf16)
-    coef_high = coef.astype(bf16)
-    coef_rest = coef - coef_high.astype(f32)
-    coef_mid = coef_rest.astype(bf16)
-    coef_low = (coef_rest - coef_mid.astype(f32)).astype(bf16)
-    edge_coef = dot(relation, coef_high) + dot(relation, coef_mid) + dot(relation, coef_low)
-    images = [
-        dot(edge_input, basis[:, b * width : (b + 1) * width]) for b in range(basis_count)
-    ]
-    message = sum(edge_coef[:, b : b + 1] * images[b] for b in range(basis_count))
-    degree = 1.0 + jnp.sum(target.astype(f32), axis=0)
-    self_part = dot(state, self_weight)
-    summed = (split_dot(target, message) + self_part) / degree[:, None]
-    aggregated = jnp.tanh(summed)
-    gate_open = jax.nn.sigmoid(dot(state, gate_weight) + gate_bias)
-    keep = 1.0 - gate_open
-    row_factor = gate_open * (1.0 - aggregated * aggregated) / degree[:, None]
-    gate_factor = (aggregated - state.astype(f32)) * gate_open * keep
-
-    basis_t = jnp.stack(
-        [basis[:, b * width : (b + 1) * width].T for b in range(basis_count)], axis=0
-    )
-    slot_ids = jnp.arange(slots, dtype=jnp.int32)[:, None]
-    row_ids = jnp.arange(rows, dtype=jnp.int32)[:, None]
-    relation_ids = jnp.arange(relations, dtype=jnp.int32)[:, None]
+    ids = jnp.concatenate([export_rows, edge_src, jnp.where(live, edge_dst, -1), edge_rel], axis=0)
+    padded = jnp.pad(coef, ((0, 0), (0, 128 - basis_count)))
+    high = padded.astype(bf16)
+    rest = padded - high.astype(f32)
+    middle = rest.astype(bf16)
+    low = (rest - middle.astype(f32)).astype(bf16)
     state_grad, basis_sum, self_sum, gate_sum, rel_sum, coef_sum, bias_sum = run_chain(
-        cotangent[0], row_factor, gate_factor, keep, target,
-        (slot_ids == edge_src[0][None, :]).astype(bf16),
-        (row_ids == export_rows[0][None, :]).astype(bf16),
-        edge_coef, basis_t, self_weight.T, gate_weight.T,
-        jnp.concatenate([image.astype(bf16) for image in images], axis=1),
-        edge_input.T, state.T,
-        (relation_ids == edge_rel[0][None, :]).astype(bf16),
+        states[0], ids, ids.T, jnp.stack([high, middle, low]), gate_bias[None],
+        cotangent[0], basis, rel_emb, self_weight, gate_weight,
     )
     height = width // ent_count
     bias = jnp.concatenate([bias_sum[0], bias_sum[1, :128]])

time: 287 us -> 235 us (0.82)
  matrix products: 29.4 us -> 0 us
  local copies, waits for them, and re-layouts: 32.6 us -> 10.8 us
  Pallas kernels: 202 us -> 221 us
  other arithmetic: 13.2 us -> 2.19 us
  starting transfers between devices: 7.59 us -> 0 us
    dot_general x14 -> x0, matrix products: 29.4 us -> none  [dot(): return lax.dot_general(a, b, dims, preferred_element_type=jnp.float32)]
    pallas_call x1, Pallas kernels: 202 us -> 221 us  [run_chain(): pl.pallas_call(chain_kernel, out_shape=(shape((rows, width), f32), shape(...]
    dot_general x4 -> x0, local copies, waits for them, and re-layouts: 7.8 us -> none  [dot(): return lax.dot_general(a, b, dims, preferred_element_type=jnp.float32)]
    all_to_all x1 -> x0, starting transfers between devices: 7.59 us -> none  [per_device(): lax.all_to_all(dot(exported, state).astype(bf16), 'ent', split_axis=0, co...]
    convert_element_type x4 -> x0, other arithmetic: 7.38 us -> none  [the longest x1 2.26 us: per_device(): (row_ids == export_rows[0][None, :]).astype(bf16)]
    unnamed x66 -> x17, local copies, waits for them, and re-layouts: 14 us -> 7.77 us
    sub x1 -> x0, local copies, waits for them, and re-layouts: 3.04 us -> none  [per_device(): keep = 1.0 - gate_open]
    div x1 -> x0, local copies, waits for them, and re-layouts: 2.9 us -> none  [per_device(): row_factor = gate_open * (1.0 - aggregated * aggregated) / degree[:, None]]
  transfers between devices with their start and end apart: 1 -> 0, of which waited for: 0 -> 0; matrix products, arithmetic and copies ran while one was open for 6% -> 0% of each run, Pallas kernels for 0% -> 0%
where the time goes in v4:
time: 235 us
  Pallas kernels  221 us (94%)
  local copies, waits for them, and re-layouts  10.8 us (5%)
    pallas_call x1, Pallas kernels, run_chain(): pl.pallas_call(chain_kernel, out_shape=(shape((rows, width), f32), shape(...  221 us
    unnamed x17, local copies, waits for them, and re-layouts  7.77 us

profile of v4, /device:TPU:64, one launch (start us, length us, event | category | flops | bytes accessed | tf_op | source)
XLA Modules:
  0.0 234.9 jit_solution(13955442850801611664)
XLA Ops:
  0.6 0.8 copy.31
  1.5 0.7 pad_maximum_fusion.coef_parts
  2.9 0.7 compare_select_fusion
  3.6 0.7 pad_add_fusion.ids_row
  4.3 0.0 copy-start
  4.3 1.0 copy.30
  5.4 0.0 copy-done
  5.4 220.6 %shard_map.180 = (f32[1024,512]{1,0:T(8,128)}, f32[16,2048]{1,0:T(8,128)}, f32[16,512]{1,0:T(8,128)}, f32[16,512]{1,0:T(8,128)}, f32[8,512]{1,0:T(8,128)}, /*index=5*/f32[8,128]{1,0:T(8,128)}, f32[8,384]{1,0:T(8,128)}) custom-call(bf16[1024,512]{1,0:T(8,128)(2,1)} %bitcast.18, s32[4,1024]{1,0:T(4,128)} %copy-done, s32[1024,4]{1,0:T(8,128)} %bitcast.16, ...), custom_call_target="tpu_custom_call" | custom-call | tf_op jit(solution)/shard_map/pallas_call | solution.py:464
  226.0 0.7 slice_reduce_fusion
  226.7 0.7 slice_bitcast_fusion
  227.4 0.6 dynamic_slice.3
  228.0 1.3 copy.32
  229.3 0.0 copy-start.1
  229.3 0.0 copy-start.3
  229.3 0.0 copy-start.2
  229.3 0.0 copy-start.4
  229.3 3.1 %copy.39 = f32[1,1024,512]{2,1,0:T(8,128)} copy(f32[1,1024,512]{2,1,0:T(8,128)} %bitcast.17) | data formatting | bytes 4194304
  232.4 0.0 copy-done.1
  232.4 0.7 copy.40
  233.1 0.0 copy-done.3
  233.1 0.6 copy.41
  233.7 0.0 copy-done.2
  233.7 0.6 copy.42
  234.3 0.0 copy-done.4
  234.3 0.6 copy.43
  (3 shorter events, 0.1 us)
Async XLA Ops:
  4.3 1.0 copy-start
  229.3 3.1 %copy-start.1 = (f32[16,2048]{1,0:T(8,128)S(1)}, f32[16,2048]{1,0:T(8,128)}, u32[]{:S(2)}) copy-start(f32[16,2048]{1,0:T(8,128)} %get-tuple-element.45) | copy-start | bytes 393220
  229.3 3.8 %copy-start.3 = (f32[16,512]{1,0:T(8,128)S(1)}, f32[16,512]{1,0:T(8,128)}, u32[]{:S(2)}) copy-start(f32[16,512]{1,0:T(8,128)} %get-tuple-element.46) | copy-start | bytes 98308
  229.3 4.4 %copy-start.2 = (f32[16,512]{1,0:T(8,128)S(1)}, f32[16,512]{1,0:T(8,128)}, u32[]{:S(2)}) copy-start(f32[16,512]{1,0:T(8,128)} %get-tuple-element.47) | copy-start | bytes 98308
  229.3 5.0 %copy-start.4 = (f32[8,512]{1,0:T(8,128)S(1)}, f32[8,512]{1,0:T(8,128)}, u32[]{:S(2)}) copy-start(f32[8,512]{1,0:T(8,128)} %get-tuple-element.50) | copy-start | bytes 49156

commit v5 on v4

--- a/solution.py
+++ b/solution.py
@@ -7,10 +7,11 @@
 
 TILE = 128
 MESH = pl.DeviceIdType.MESH
-CHUNKS = 2
+CHUNKS = 4
 BLOCK = 256
 SIDE = 4
 GROUP = 16
+PIECES = 4
 EXPORT, SOURCE, TARGET, RELATION = range(4)
 LAST = (((1,), (1,)), ((), ()))
 
@@ -232,36 +233,6 @@
 
         lax.fori_loop(1, ents, send, 0)
 
-    def local_part(r):
-        state_grad[r, :] += dot(row_grad[r, :], self_weight[...], LAST) + dot(
-            gate_row[r, :], gate_weight[...], LAST
-        )
-        exported_t[r, :] = by_column(EXPORT, r)
-
-    blocks(rows, local_part)
-
-    for c in range(CHUNKS):
-        cols = pl.ds(c * part, part)
-        pltpu.make_async_copy(slot_recv.at[c], slot_recv.at[c], a_recv_sem.at[c]).wait()
-
-        def to_rows(r):
-            out = state_grad[r, cols] + dot(exported_t[r, :], slot_recv[c])
-            state_grad[r, cols] = out
-            sending[c, r, :] = out.astype(bf16)
-
-        blocks(rows, to_rows)
-
-        @pl.when(t > 0)
-        def _():
-            pass_down(c).start()
-
-    def turn(r):
-        input_t[:, r] = edge_input[r, :].T
-        state_t[:, r] = state[r, :].T
-
-    blocks(edges, turn)
-    relation_line = lax.broadcasted_iota(jnp.int32, (relations, edges), 0)
-    relation_t[...] = one(ids_row[RELATION : RELATION + 1, :] == relation_line)
     core = lax.rem(me, 2)
     y = lax.rem(me // 2, SIDE)
     x = me // (2 * SIDE)
@@ -297,46 +268,85 @@
         lax.fori_loop(0, SIDE, step, 0)
         to_pair(offset).start()
 
-    for b in range(basis_count):
-
-        def scale(e):
-            scaled[e, :] = (edge_coef[e, b : b + 1] * edge_grad[e, :].astype(f32)).astype(bf16)
-
-        blocks(edges, scale)
-        term(b * GROUP, input_t, scaled)
-    term(basis_count * GROUP, state_t, row_grad)
-    term((basis_count + 1) * GROUP, state_t, gate_row)
-
-    def inner(e):
-        lane = lax.broadcasted_iota(jnp.int32, (BLOCK, 128), 1)
-        out = jnp.zeros((BLOCK, 128), f32)
-        gradient = edge_grad[e, :].astype(f32)
+    def weights():
+        def turn(r):
+            input_t[:, r] = edge_input[r, :].T
+            state_t[:, r] = state[r, :].T
+
+        blocks(edges, turn)
+        relation_line = lax.broadcasted_iota(jnp.int32, (relations, edges), 0)
+        relation_t[...] = one(ids_row[RELATION : RELATION + 1, :] == relation_line)
         for b in range(basis_count):
-            product = gradient * images[e, b * width : (b + 1) * width].astype(f32)
-            out = jnp.where(lane == b, jnp.sum(product, axis=1, keepdims=True), out)
-        high = out.astype(bf16)
-        coef_hi[e, :] = high
-        coef_lo[e, :] = (out - high.astype(f32)).astype(bf16)
-
-    blocks(edges, inner)
-    bias = jnp.zeros((1, width), f32)
-    for i in range(rows // BLOCK):
-        piece = gate_row[i * BLOCK : (i + 1) * BLOCK, :].astype(f32)
-        bias = bias + jnp.sum(piece, axis=0, keepdims=True)
-    line = lax.broadcasted_iota(jnp.int32, (8, width - 128), 0)
-    wrapped = jnp.concatenate([bias[:, width - 128 :]] * (width // 128 - 1), axis=1)
-    tile = jnp.where(line == 0, bias[:, : width - 128], jnp.where(line == 1, wrapped, 0.0))
-    small[:, 0:8, :] = dot(relation_t[...], input_grad[...]).reshape(ents, 8, width)
-    coef_rows = dot(relation_t[...], coef_hi[...]) + dot(relation_t[...], coef_lo[...])
-    small[:, 8:16, 0:128] = coef_rows.reshape(ents, 8, 128)
-    small[:, 8:16, 128:] = jnp.broadcast_to(tile[None], (ents, 8, width - 128))
-
-    def pack_small(i, carry):
-        pack((basis_count + 2) * GROUP, i, small[pl.ds(i * 2 * SIDE, 2 * SIDE)])
-        return carry
-
-    lax.fori_loop(0, SIDE, pack_small, 0)
-    to_pair((basis_count + 2) * GROUP).start()
+
+            def scale(e):
+                scaled[e, :] = (edge_coef[e, b : b + 1] * edge_grad[e, :].astype(f32)).astype(bf16)
+
+            blocks(edges, scale)
+            term(b * GROUP, input_t, scaled)
+        term(basis_count * GROUP, state_t, row_grad)
+        term((basis_count + 1) * GROUP, state_t, gate_row)
+
+        def inner(e):
+            lane = lax.broadcasted_iota(jnp.int32, (BLOCK, 128), 1)
+            out = jnp.zeros((BLOCK, 128), f32)
+            gradient = edge_grad[e, :].astype(f32)
+            for b in range(basis_count):
+                product = gradient * images[e, b * width : (b + 1) * width].astype(f32)
+                out = jnp.where(lane == b, jnp.sum(product, axis=1, keepdims=True), out)
+            high = out.astype(bf16)
+            coef_hi[e, :] = high
+            coef_lo[e, :] = (out - high.astype(f32)).astype(bf16)
+
+        blocks(edges, inner)
+        bias = jnp.zeros((1, width), f32)
+        for i in range(rows // BLOCK):
+            piece = gate_row[i * BLOCK : (i + 1) * BLOCK, :].astype(f32)
+            bias = bias + jnp.sum(piece, axis=0, keepdims=True)
+        line = lax.broadcasted_iota(jnp.int32, (8, width - 128), 0)
+        wrapped = jnp.concatenate([bias[:, width - 128 :]] * (width // 128 - 1), axis=1)
+        tile = jnp.where(line == 0, bias[:, : width - 128], jnp.where(line == 1, wrapped, 0.0))
+        small[:, 0:8, :] = dot(relation_t[...], input_grad[...]).reshape(ents, 8, width)
+        coef_rows = dot(relation_t[...], coef_hi[...]) + dot(relation_t[...], coef_lo[...])
+        small[:, 8:16, 0:128] = coef_rows.reshape(ents, 8, 128)
+        small[:, 8:16, 128:] = jnp.broadcast_to(tile[None], (ents, 8, width - 128))
+
+        def pack_small(i, carry):
+            pack((basis_count + 2) * GROUP, i, small[pl.ds(i * 2 * SIDE, 2 * SIDE)])
+            return carry
+
+        lax.fori_loop(0, SIDE, pack_small, 0)
+        to_pair((basis_count + 2) * GROUP).start()
+
+    def local_part(r):
+        state_grad[r, :] += dot(row_grad[r, :], self_weight[...], LAST) + dot(
+            gate_row[r, :], gate_weight[...], LAST
+        )
+        exported_t[r, :] = by_column(EXPORT, r)
+
+    blocks(rows, local_part)
+
+    @pl.when(t == 0)
+    def _():
+        weights()
+
+    for c in range(CHUNKS):
+        cols = pl.ds(c * part, part)
+        pltpu.make_async_copy(slot_recv.at[c], slot_recv.at[c], a_recv_sem.at[c]).wait()
+
+        def to_rows(r):
+            out = state_grad[r, cols] + dot(exported_t[r, :], slot_recv[c])
+            state_grad[r, cols] = out
+            sending[c, r, :] = out.astype(bf16)
+
+        blocks(rows, to_rows)
+
+        @pl.when(t > 0)
+        def _():
+            pass_down(c).start()
+
+    @pl.when(t > 0)
+    def _():
+        weights()
 
     pltpu.make_async_copy(pair_recv, pair_recv, pair_sem.at[1]).wait()
 
@@ -511,6 +521,29 @@
     )(*operands)
 
 
+def write_kernel(*refs):
+    count = len(refs) // 2
+    refs[count][...] = refs[0][...]
+
+    @pl.when(pl.program_id(0) == 0)
+    def _():
+        for i in range(1, count):
+            refs[count + i][...] = refs[i][...]
+
+
+def write_out(*arrays):
+    rows, width = arrays[0].shape
+    specs = [pl.BlockSpec((rows // PIECES, width), lambda i: (i, 0))]
+    specs += [pl.BlockSpec(array.shape, lambda i: (0, 0)) for array in arrays[1:]]
+    return pl.pallas_call(
+        write_kernel,
+        grid=(PIECES,),
+        out_shape=tuple(jax.ShapeDtypeStruct(array.shape, array.dtype) for array in arrays),
+        in_specs=specs,
+        out_specs=tuple(specs),
+    )(*arrays)
+
+
 def per_device(
     states, cotangent, export_rows, edge_src, edge_dst, edge_rel, tile_count,
     basis, coef, rel_emb, self_weight, gate_weight, gate_bias,
@@ -531,6 +564,9 @@
         states[0], ids, ids.T, jnp.stack([high, middle, low]), gate_bias[None],
         cotangent[0], basis, rel_emb, self_weight, gate_weight,
     )
+    state_grad, basis_sum, self_sum, gate_sum, rel_sum = write_out(
+        state_grad, basis_sum, self_sum, gate_sum, rel_sum
+    )
     height = width // ent_count
     bias = jnp.concatenate([bias_sum[0], bias_sum[1, :128]])
     return (

time: 235 us -> 221 us (0.940)
  Pallas kernels: 221 us -> 213 us
  local copies, waits for them, and re-layouts: 10.8 us -> 4.51 us
    pallas_call x1, Pallas kernels: 221 us -> 209 us  [run_chain(): pl.pallas_call(chain_kernel, out_shape=(shape((rows, width), f32), shape(...]
    unnamed x17 -> x6, local copies, waits for them, and re-layouts: 7.77 us -> 1.48 us
    pallas_call x0 -> x1, Pallas kernels: none -> 3.91 us  [write_out(): pl.pallas_call(write_kernel, grid=(PIECES,), out_shape=tuple((jax.ShapeDt...]
where the time goes in v5:
time: 221 us
  Pallas kernels  213 us (96%)
  local copies, waits for them, and re-layouts  4.51 us (2%)
    pallas_call x1, Pallas kernels, run_chain(): pl.pallas_call(chain_kernel, out_shape=(shape((rows, width), f32), shape(...  209 us

profile of v5, /device:TPU:64, one launch (start us, length us, event | category | flops | bytes accessed | tf_op | source)
XLA Modules:
  0.0 220.9 jit_solution(10275767507584794086)
XLA Ops:
  0.6 0.8 copy.31
  1.5 0.7 pad_maximum_fusion.coef_parts
  2.9 0.7 compare_select_fusion
  3.6 0.7 pad_add_fusion.ids_row
  4.3 0.0 copy-start
  4.3 1.0 copy.30
  5.4 0.0 copy-done
  5.4 209.0 %shard_map.180 = (f32[1024,512]{1,0:T(8,128)}, f32[16,2048]{1,0:T(8,128)}, f32[16,512]{1,0:T(8,128)}, f32[16,512]{1,0:T(8,128)}, f32[8,512]{1,0:T(8,128)}, /*index=5*/f32[8,128]{1,0:T(8,128)}, f32[8,384]{1,0:T(8,128)}) custom-call(bf16[1024,512]{1,0:T(8,128)(2,1)} %bitcast.17, s32[4,1024]{1,0:T(4,128)} %copy-done, s32[1024,4]{1,0:T(8,128)} %bitcast.16, ...), custom_call_target="tpu_custom_call" | custom-call | tf_op jit(solution)/shard_map/pallas_call | solution.py:474
  214.3 0.0 copy-start.1
  214.3 3.9 %shard_map.181 = (f32[1024,512]{1,0:T(8,128)}, f32[16,2048]{1,0:T(8,128)}, f32[16,512]{1,0:T(8,128)}, f32[16,512]{1,0:T(8,128)}, f32[8,512]{1,0:T(8,128)}) custom-call(f32[1024,512]{1,0:T(8,128)} %get-tuple-element.19.refs_0_, f32[16,2048]{1,0:T(8,128)} %get-tuple-element.20.refs_1_, f32[16,512]{1,0:T(8,128)} %get-tuple-element.21.refs_2_, ...), custom_call_target="tpu_custom_call" | custom-call | tf_op jit(solution)/shard_map/pallas_call | solution.py:538
  218.3 0.7 slice_reduce_fusion
  219.0 0.7 slice_bitcast_fusion
  219.7 0.6 dynamic_slice.3
  220.3 0.0 copy-done.1
  220.3 0.7 copy.32
  (3 shorter events, 0.1 us)
Async XLA Ops:
  4.3 1.0 copy-start
  214.3 5.9 %copy-start.1 = (f32[8,128]{1,0:T(8,128)S(1)}, f32[8,128]{1,0:T(8,128)}, u32[]{:S(2)}) copy-start(f32[8,128]{1,0:T(8,128)} %get-tuple-element.29) | copy-start | bytes 12292

commit v6 on v5

--- a/solution.py
+++ b/solution.py
@@ -8,10 +8,11 @@
 TILE = 128
 MESH = pl.DeviceIdType.MESH
 CHUNKS = 4
-BLOCK = 256
+BLOCK = 512
 SIDE = 4
 GROUP = 16
 PIECES = 4
+LONG_WAY = (256, 256, 256, 128)
 EXPORT, SOURCE, TARGET, RELATION = range(4)
 LAST = (((1,), (1,)), ((), ()))
 
@@ -28,10 +29,10 @@
     row_factor, gate_factor, keep, target, source_t, early, exported_t, edge_coef,
     export_send, export_recv, edge_input,
     row_grad, gate_row, edge_grad, input_grad,
-    handed, sending, total, slot_send, slot_recv,
+    handed, sending, relay, total, slot_send, slot_recv,
     images, input_t, state_t, relation_t, scaled, coef_hi, coef_lo, small,
     packed, pair_recv, first_recv, first_sum, second_recv, shares,
-    z_send_sem, z_recv_sem, a_send_sem, a_recv_sem, load_sem, export_sem,
+    z_send_sem, z_recv_sem, hop_send_sem, hop_recv_sem, a_send_sem, a_recv_sem, load_sem, export_sem,
     pair_sem, first_send_sem, first_recv_sem, second_send_sem, second_recv_sem, share_sem,
 ):
     bf16, f32 = jnp.bfloat16, jnp.float32
@@ -74,14 +75,39 @@
         load.start()
 
     def pass_down(c):
+        piece = pl.ds(0, rows - LONG_WAY[c])
         return pltpu.make_async_remote_copy(
-            src_ref=sending.at[c],
-            dst_ref=handed.at[c],
+            src_ref=sending.at[c, piece],
+            dst_ref=handed.at[c, piece],
             send_sem=z_send_sem.at[c],
             recv_sem=z_recv_sem.at[c],
             device_id=(below, me),
             device_id_type=MESH,
         )
+
+    def hop(c, leg):
+        count = LONG_WAY[c]
+        piece, held = pl.ds(rows - count, count), pl.ds(0, count)
+        stops = [
+            sending.at[c, piece], relay.at[0, c, held], relay.at[1, c, held], handed.at[c, piece]
+        ]
+        return pltpu.make_async_remote_copy(
+            src_ref=stops[leg],
+            dst_ref=stops[leg + 1],
+            send_sem=hop_send_sem.at[leg, c],
+            recv_sem=hop_recv_sem.at[leg, c],
+            device_id=(above, me),
+            device_id_type=MESH,
+        )
+
+    detours = [c for c in range(CHUNKS) if LONG_WAY[c] > 0]
+
+    def pass_on(leg):
+        for c in detours:
+            hop(c, leg - 1).wait_recv()
+            hop(c, leg).start()
+        for c in detours:
+            hop(c, leg).wait_send()
 
     def blocks(count, body):
         def step(i, carry):
@@ -172,12 +198,22 @@
     blocks(rows, factors)
     loads[4].wait()
 
+    @pl.when(t == 0)
+    def _():
+        pass_on(1)
+
+    @pl.when(t <= 1)
+    def _():
+        pass_on(2)
+
     for c in range(CHUNKS):
         cols = pl.ds(c * part, part)
 
         @pl.when(t < sections - 1)
         def _():
             pass_down(c).wait_recv()
+            if c in detours:
+                hop(c, 2).wait_recv()
 
         @pl.when(t == sections - 1)
         def _():
@@ -325,28 +361,39 @@
 
     blocks(rows, local_part)
 
+    def finish_rows(last):
+        for c in range(CHUNKS):
+            cols = pl.ds(c * part, part)
+            pltpu.make_async_copy(slot_recv.at[c], slot_recv.at[c], a_recv_sem.at[c]).wait()
+
+            def to_rows(r):
+                out = state_grad[r, cols] + dot(exported_t[r, :], slot_recv[c])
+                state_grad[r, cols] = out
+                if not last:
+                    sending[c, r, :] = out.astype(bf16)
+
+            blocks(rows, to_rows)
+            if not last:
+                if c in detours:
+                    hop(c, 0).start()
+                pass_down(c).start()
+
     @pl.when(t == 0)
     def _():
         weights()
 
-    for c in range(CHUNKS):
-        cols = pl.ds(c * part, part)
-        pltpu.make_async_copy(slot_recv.at[c], slot_recv.at[c], a_recv_sem.at[c]).wait()
-
-        def to_rows(r):
-            out = state_grad[r, cols] + dot(exported_t[r, :], slot_recv[c])
-            state_grad[r, cols] = out
-            sending[c, r, :] = out.astype(bf16)
-
-        blocks(rows, to_rows)
-
-        @pl.when(t > 0)
-        def _():
-            pass_down(c).start()
-
     @pl.when(t > 0)
     def _():
+        finish_rows(False)
         weights()
+
+    @pl.when(t >= 2)
+    def _():
+        pass_on(1)
+
+    @pl.when(t == 3)
+    def _():
+        pass_on(2)
 
     pltpu.make_async_copy(pair_recv, pair_recv, pair_sem.at[1]).wait()
 
@@ -374,6 +421,10 @@
                 device_id=chip(to, y) if h == 0 else chip(x, to),
                 device_id_type=MESH,
             ).start()
+
+    @pl.when(t == 0)
+    def _():
+        finish_rows(True)
 
     for h in range(2):
         pltpu.make_async_copy(first_recv.at[h], first_recv.at[h], first_recv_sem.at[h]).wait()
@@ -450,6 +501,8 @@
         @pl.when(t > 0)
         def _():
             pass_down(c).wait_send()
+            if c in detours:
+                hop(c, 0).wait_send()
 
 
 def run_chain(*operands):
@@ -462,6 +515,7 @@
     part, half = width // CHUNKS, width // 2
     height = (basis_count + 3) * GROUP
     shape = jax.ShapeDtypeStruct
+    hop_sem = pltpu.SemaphoreType.DMA((3, CHUNKS))
     chunk_sem = pltpu.SemaphoreType.DMA((CHUNKS,))
     two = pltpu.SemaphoreType.DMA((2,))
     whole = pl.BlockSpec(memory_space=pltpu.VMEM)
@@ -496,6 +550,7 @@
             flat, flat, flat, flat,
             pltpu.VMEM((CHUNKS, rows, part), bf16),
             pltpu.VMEM((CHUNKS, rows, part), bf16),
+            pltpu.VMEM((2, CHUNKS, max(LONG_WAY), part), bf16),
             wide,
             pltpu.VMEM((CHUNKS, slots, part), bf16),
             pltpu.VMEM((CHUNKS, slots, part), bf16),
@@ -511,7 +566,7 @@
             pltpu.VMEM((2, SIDE, height, half), bf16),
             pltpu.VMEM((2, SIDE - 1, height, half), bf16),
             pltpu.VMEM((SIDE, 2, height, half), bf16),
-            chunk_sem, chunk_sem, chunk_sem, chunk_sem,
+            chunk_sem, chunk_sem, hop_sem, hop_sem, chunk_sem, chunk_sem,
             pltpu.SemaphoreType.DMA((5,)),
             two, two, two, two, two, two, two,
         ],

time: 221 us -> 203 us (0.919)
  Pallas kernels: 213 us -> 195 us
    pallas_call x1, Pallas kernels: 209 us -> 191 us  [run_chain(): pl.pallas_call(chain_kernel, out_shape=(shape((rows, width), f32), shape(...]
where the time goes in v6:
time: 203 us
  Pallas kernels  195 us (96%)
  local copies, waits for them, and re-layouts  4.51 us (2%)
  other arithmetic  2.18 us (1%)
    pallas_call x1, Pallas kernels, run_chain(): pl.pallas_call(chain_kernel, out_shape=(shape((rows, width), f32), shape(...  191 us

profile of v6, /device:TPU:64, one launch (start us, length us, event | category | flops | bytes accessed | tf_op | source)
XLA Modules:
  0.0 202.9 jit_solution(7731197820201296174)
XLA Ops:
  0.6 0.8 copy.31
  1.5 0.7 pad_maximum_fusion.coef_parts
  2.9 0.7 compare_select_fusion
  3.6 0.7 pad_add_fusion.ids_row
  4.3 0.0 copy-start
  4.3 1.0 copy.30
  5.4 0.0 copy-done
  5.4 190.9 %shard_map.180 = (f32[1024,512]{1,0:T(8,128)}, f32[16,2048]{1,0:T(8,128)}, f32[16,512]{1,0:T(8,128)}, f32[16,512]{1,0:T(8,128)}, f32[8,512]{1,0:T(8,128)}, /*index=5*/f32[8,128]{1,0:T(8,128)}, f32[8,384]{1,0:T(8,128)}) custom-call(bf16[1024,512]{1,0:T(8,128)(2,1)} %bitcast.17, s32[4,1024]{1,0:T(4,128)} %copy-done, s32[1024,4]{1,0:T(8,128)} %bitcast.16, ...), custom_call_target="tpu_custom_call" | custom-call | tf_op jit(solution)/shard_map/pallas_call | solution.py:528
  196.3 0.0 copy-start.1
  196.3 3.9 %shard_map.181 = (f32[1024,512]{1,0:T(8,128)}, f32[16,2048]{1,0:T(8,128)}, f32[16,512]{1,0:T(8,128)}, f32[16,512]{1,0:T(8,128)}, f32[8,512]{1,0:T(8,128)}) custom-call(f32[1024,512]{1,0:T(8,128)} %get-tuple-element.19.refs_0_, f32[16,2048]{1,0:T(8,128)} %get-tuple-element.20.refs_1_, f32[16,512]{1,0:T(8,128)} %get-tuple-element.21.refs_2_, ...), custom_call_target="tpu_custom_call" | custom-call | tf_op jit(solution)/shard_map/pallas_call | solution.py:593
  200.2 0.7 slice_reduce_fusion
  200.9 0.7 slice_bitcast_fusion
  201.6 0.6 dynamic_slice.3
  202.2 0.0 copy-done.1
  202.2 0.7 copy.32
  (3 shorter events, 0.1 us)
Async XLA Ops:
  4.3 1.0 copy-start
  196.3 5.9 %copy-start.1 = (f32[8,128]{1,0:T(8,128)S(1)}, f32[8,128]{1,0:T(8,128)}, u32[]{:S(2)}) copy-start(f32[8,128]{1,0:T(8,128)} %get-tuple-element.29) | copy-start | bytes 12292

commit v7 on v6

--- a/solution.py
+++ b/solution.py
@@ -22,12 +22,12 @@
 
 
 def chain_kernel(
-    state, ids_row, ids_col, coef_parts, gate_bias,
+    state, export_rows, edge_src, edge_dst, edge_rel, tile_count, coef_t, gate_bias,
     cot_hbm, basis_hbm, rel_emb_hbm, self_hbm, gate_hbm,
     state_grad, basis_out, self_out, gate_out, rel_out, coef_out, bias_out,
     cot, basis, rel_emb, self_weight, gate_weight,
     row_factor, gate_factor, keep, target, source_t, early, exported_t, edge_coef,
-    export_send, export_recv, edge_input,
+    export_send, export_recv, edge_input, ids_row, ids_col, coef_rows_in, coef_parts,
     row_grad, gate_row, edge_grad, input_grad,
     handed, sending, relay, total, slot_send, slot_recv,
     images, input_t, state_t, relation_t, scaled, coef_hi, coef_lo, small,
@@ -39,7 +39,7 @@
     t, me = lax.axis_index("tm"), lax.axis_index("ent")
     sections, ents = lax.axis_size("tm"), lax.axis_size("ent")
     rows, width = state.shape
-    edges = slots = ids_row.shape[1]
+    edges = slots = export_rows.shape[1]
     relations = rel_emb.shape[0]
     basis_count = basis.shape[1] // width
     share = slots // ents
@@ -116,6 +116,14 @@
 
         lax.fori_loop(0, count // BLOCK, step, 0)
 
+    ids_row[...] = jnp.zeros_like(ids_row)
+    live = lax.broadcasted_iota(jnp.int32, (1, edges), 1) < tile_count[...] * TILE
+    ids_row[EXPORT : EXPORT + 1, :] = export_rows[...]
+    ids_row[SOURCE : SOURCE + 1, :] = edge_src[...]
+    ids_row[TARGET : TARGET + 1, :] = jnp.where(live, edge_dst[...], -1)
+    ids_row[RELATION : RELATION + 1, :] = edge_rel[...]
+    ids_col[...] = ids_row[...].T
+
     def one(mask):
         return jnp.where(mask, 1.0, 0.0).astype(bf16)
 
@@ -151,13 +159,23 @@
     lax.fori_loop(1, ents, send_export, 0)
     for load in loads[:3]:
         load.wait()
+    coef_parts[...] = jnp.zeros_like(coef_parts)
+    coef_rows_in[...] = jnp.zeros_like(coef_rows_in)
+    coef_rows_in[:basis_count, :] = coef_t[...]
+    left_over = coef_rows_in[...].T
+    for i in range(3):
+        kept = left_over.astype(bf16).astype(f32)
+        coef_parts[i, :, :8] = kept
+        left_over = left_over - kept
 
     def by_edge(e):
         early[e, :] = by_row(SOURCE, e, slots)
         target[e, :] = by_row(TARGET, e, rows)
         relation = by_row(RELATION, e, relations)
         total[e, :] = dot(relation, rel_emb[...])
-        edge_coef[e, :] = sum(dot(relation, coef_parts[i]) for i in range(3))
+        edge_coef[e, :] = sum(
+            dot(relation, coef_parts[i].astype(bf16)) for i in range(3)
+        )
 
     blocks(edges, by_edge)
 
@@ -197,6 +215,19 @@
 
     blocks(rows, factors)
     loads[4].wait()
+
+    def turned():
+        def turn(r):
+            input_t[:, r] = edge_input[r, :].T
+            state_t[:, r] = state[r, :].T
+
+        blocks(edges, turn)
+        relation_line = lax.broadcasted_iota(jnp.int32, (relations, edges), 0)
+        relation_t[...] = one(ids_row[RELATION : RELATION + 1, :] == relation_line)
+
+    @pl.when(t < sections - 1)
+    def _():
+        turned()
 
     @pl.when(t == 0)
     def _():
@@ -296,22 +327,16 @@
                 packed[core_to, 1, y_to * SIDE + i, rows_at, :] = one[:, half:]
 
     def term(offset, left, right):
-        def step(i, carry):
-            r = pl.ds(pl.multiple_of(i * 128, 128), 128)
-            pack(offset, i, dot(left[r, :], right[...]))
-            return carry
-
-        lax.fori_loop(0, SIDE, step, 0)
+        value = dot(left[...], right[...])
+        for i in range(SIDE):
+            pack(offset, i, value[i * 128 : (i + 1) * 128])
         to_pair(offset).start()
 
     def weights():
-        def turn(r):
-            input_t[:, r] = edge_input[r, :].T
-            state_t[:, r] = state[r, :].T
-
-        blocks(edges, turn)
-        relation_line = lax.broadcasted_iota(jnp.int32, (relations, edges), 0)
-        relation_t[...] = one(ids_row[RELATION : RELATION + 1, :] == relation_line)
+        @pl.when(t == sections - 1)
+        def _():
+            turned()
+
         for b in range(basis_count):
 
             def scale(e):
@@ -359,9 +384,8 @@
         )
         exported_t[r, :] = by_column(EXPORT, r)
 
-    blocks(rows, local_part)
-
     def finish_rows(last):
+        blocks(rows, local_part)
         for c in range(CHUNKS):
             cols = pl.ds(c * part, part)
             pltpu.make_async_copy(slot_recv.at[c], slot_recv.at[c], a_recv_sem.at[c]).wait()
@@ -509,8 +533,7 @@
     bf16, f32 = jnp.bfloat16, jnp.float32
     rows, width = operands[0].shape
     edges = slots = operands[1].shape[1]
-    basis_count = operands[6].shape[1] // width
-    relations = operands[7].shape[0]
+    basis_count, relations = operands[6].shape
     ents = lax.axis_size("ent")
     part, half = width // CHUNKS, width // 2
     height = (basis_count + 3) * GROUP
@@ -536,7 +559,7 @@
             shape((8, 128), f32),
             shape((8, width - 128), f32),
         ),
-        in_specs=[whole] * 5 + [pl.BlockSpec(memory_space=pl.ANY)] * 5,
+        in_specs=[whole] * 8 + [pl.BlockSpec(memory_space=pl.ANY)] * 5,
         out_specs=(whole,) * 7,
         scratch_shapes=[
             flat,
@@ -547,6 +570,10 @@
             wide, wide, wide, hot, hot, hot, hot,
             pltpu.VMEM((edges, 128), f32),
             flat, flat, flat,
+            pltpu.VMEM((8, edges), jnp.int32),
+            pltpu.VMEM((edges, 8), jnp.int32),
+            pltpu.VMEM((8, relations), f32),
+            pltpu.VMEM((3, relations, 128), f32),
             flat, flat, flat, flat,
             pltpu.VMEM((CHUNKS, rows, part), bf16),
             pltpu.VMEM((CHUNKS, rows, part), bf16),
@@ -582,20 +609,33 @@
 
     @pl.when(pl.program_id(0) == 0)
     def _():
-        for i in range(1, count):
+        for i in range(1, count - 2):
             refs[count + i][...] = refs[i][...]
-
-
-def write_out(*arrays):
+        coef_in, bias_in, coef_out, bias_out = (refs[i] for i in (count - 2, count - 1, -2, -1))
+        coef_out[...] = coef_in[...].T[: coef_out.shape[0]]
+        bias = bias_in[...]
+        bias = jnp.concatenate([bias, jnp.roll(bias[:, :128], -1, axis=0)], axis=1)
+        width = bias.shape[1]
+        share = bias_out.shape[1]
+        shift = lax.rem(width - lax.axis_index("ent") * share, width)
+        bias_out[...] = pltpu.roll(bias, shift, 1)[:1, :share]
+
+
+def write_out(basis_count, *arrays):
     rows, width = arrays[0].shape
-    specs = [pl.BlockSpec((rows // PIECES, width), lambda i: (i, 0))]
-    specs += [pl.BlockSpec(array.shape, lambda i: (0, 0)) for array in arrays[1:]]
+    shapes = [array.shape for array in arrays]
+    results = shapes[:-2] + [(basis_count, 8), (1, width // lax.axis_size("ent"))]
+
+    def specs(sizes):
+        rest = [pl.BlockSpec(size, lambda i: (0, 0)) for size in sizes[1:]]
+        return [pl.BlockSpec((rows // PIECES, width), lambda i: (i, 0))] + rest
+
     return pl.pallas_call(
         write_kernel,
         grid=(PIECES,),
-        out_shape=tuple(jax.ShapeDtypeStruct(array.shape, array.dtype) for array in arrays),
-        in_specs=specs,
-        out_specs=tuple(specs),
+        out_shape=tuple(jax.ShapeDtypeStruct(size, jnp.float32) for size in results),
+        in_specs=specs(shapes),
+        out_specs=tuple(specs(results)),
     )(*arrays)
 
 
@@ -603,36 +643,13 @@
     states, cotangent, export_rows, edge_src, edge_dst, edge_rel, tile_count,
     basis, coef, rel_emb, self_weight, gate_weight, gate_bias,
 ):
-    bf16, f32 = jnp.bfloat16, jnp.float32
-    ent_count = lax.axis_size("ent")
-    width = states.shape[2]
-    basis_count = basis.shape[1] // width
-    edges = edge_src.shape[1]
-    live = jnp.arange(edges, dtype=jnp.int32) // TILE < tile_count[0, 0]
-    ids = jnp.concatenate([export_rows, edge_src, jnp.where(live, edge_dst, -1), edge_rel], axis=0)
-    padded = jnp.pad(coef, ((0, 0), (0, 128 - basis_count)))
-    high = padded.astype(bf16)
-    rest = padded - high.astype(f32)
-    middle = rest.astype(bf16)
-    low = (rest - middle.astype(f32)).astype(bf16)
-    state_grad, basis_sum, self_sum, gate_sum, rel_sum, coef_sum, bias_sum = run_chain(
-        states[0], ids, ids.T, jnp.stack([high, middle, low]), gate_bias[None],
+    basis_count = coef.shape[1]
+    sums = run_chain(
+        states[0], export_rows, edge_src, edge_dst, edge_rel, tile_count, coef.T, gate_bias[None],
         cotangent[0], basis, rel_emb, self_weight, gate_weight,
     )
-    state_grad, basis_sum, self_sum, gate_sum, rel_sum = write_out(
-        state_grad, basis_sum, self_sum, gate_sum, rel_sum
-    )
-    height = width // ent_count
-    bias = jnp.concatenate([bias_sum[0], bias_sum[1, :128]])
-    return (
-        state_grad[None],
-        basis_sum,
-        self_sum,
-        gate_sum,
-        lax.dynamic_slice_in_dim(bias, lax.axis_index("ent") * height, height, 0),
-        coef_sum[:, :basis_count],
-        rel_sum,
-    )
+    state_grad, basis_sum, self_sum, gate_sum, rel_sum, coef_t, bias = write_out(basis_count, *sums)
+    return state_grad[None], basis_sum, self_sum, gate_sum, bias[0], coef_t.T, rel_sum
 
 
 def solution(mesh):

time: 203 us -> 192 us (0.946)
  Pallas kernels: 195 us -> 190 us
  local copies, waits for them, and re-layouts: 4.51 us -> 0 us
  other arithmetic: 2.18 us -> 0 us
    pallas_call x1, Pallas kernels: 191 us -> 186 us  [run_chain(): pl.pallas_call(chain_kernel, out_shape=(shape((rows, width), f32), shape(...]
where the time goes in v7:
time: 192 us; the launch traced here: 191 us
  Pallas kernels  190 us (99%)
    pallas_call x1, Pallas kernels, run_chain(): pl.pallas_call(chain_kernel, out_shape=(shape((rows, width), f32), shape(...  186 us
    pallas_call x1, Pallas kernels, write_out(): pl.pallas_call(write_kernel, grid=(PIECES,), out_shape=tuple((jax.ShapeDt...  4.02 us

profile of v7, /device:TPU:64, one launch (start us, length us, event | category | flops | bytes accessed | tf_op | source)
XLA Modules:
  0.0 191.3 jit_solution(5547165731523809176)
XLA Ops:
  1.3 185.8 %shard_map.180 = (f32[1024,512]{1,0:T(8,128)}, f32[16,2048]{1,0:T(8,128)}, f32[16,512]{1,0:T(8,128)}, f32[16,512]{1,0:T(8,128)}, f32[8,512]{1,0:T(8,128)}, /*index=5*/f32[8,128]{1,0:T(8,128)}, f32[8,384]{1,0:T(8,128)}) custom-call(bf16[1024,512]{1,0:T(8,128)(2,1)} %bitcast.7, s32[1,1024]{1,0:T(1,128)} %export_rows.1, s32[1,1024]{1,0:T(1,128)} %edge_src.1, ...), custom_call_target="tpu_custom_call" | custom-call | tf_op jit(solution)/shard_map/pallas_call | solution.py:551
  187.1 4.0 %shard_map.181 = (f32[1024,512]{1,0:T(8,128)}, f32[16,2048]{1,0:T(8,128)}, f32[16,512]{1,0:T(8,128)}, f32[16,512]{1,0:T(8,128)}, f32[8,512]{1,0:T(8,128)}, /*index=5*/f32[4,8]{1,0:T(4,128)}, f32[1,16]{1,0:T(1,128)}) custom-call(f32[1024,512]{1,0:T(8,128)} %get-tuple-element.21.refs_0_, f32[16,2048]{1,0:T(8,128)} %get-tuple-element.22.refs_1_, ...), custom_call_target="tpu_custom_call" | custom-call | tf_op jit(solution)/shard_map/pallas_call | solution.py:633

commit v8 on v7

--- a/solution.py
+++ b/solution.py
@@ -11,7 +11,7 @@
 BLOCK = 512
 SIDE = 4
 GROUP = 16
-PIECES = 4
+PIECES = 2
 LONG_WAY = (256, 256, 256, 128)
 EXPORT, SOURCE, TARGET, RELATION = range(4)
 LAST = (((1,), (1,)), ((), ()))
@@ -261,11 +261,13 @@
         def through_basis(e):
             gathered = dot(target[e, :], row_grad[:, cols])
             edge_grad[e, cols] = gathered.astype(bf16)
-            out = 0.0
-            for b in range(basis_count):
-                image_grad = (edge_coef[e, b : b + 1] * gathered).astype(bf16)
-                at = slice(b * width + c * part, b * width + (c + 1) * part)
-                out = out + dot(image_grad, basis[:, at], LAST)
+            scales = [edge_coef[e, b : b + 1] for b in range(basis_count)]
+            image_grad = [(scale * gathered).astype(bf16) for scale in scales]
+            starts = [b * width + c * part for b in range(basis_count)]
+            columns = [basis[:, start : start + part] for start in starts]
+            out = dot(
+                jnp.concatenate(image_grad, axis=1), jnp.concatenate(columns, axis=1), LAST
+            )
             if c > 0:
                 out = out + total[e, :]
             if c < CHUNKS - 1:

time: 192 us -> 182 us (0.948)
  Pallas kernels: 190 us -> 180 us
    pallas_call x1, Pallas kernels: 186 us -> 177 us  [run_chain(): pl.pallas_call(chain_kernel, out_shape=(shape((rows, width), f32), shape(...]
where the time goes in v8:
time: 182 us
  Pallas kernels  180 us (99%)
    pallas_call x1, Pallas kernels, run_chain(): pl.pallas_call(chain_kernel, out_shape=(shape((rows, width), f32), shape(...  177 us

profile of v8, /device:TPU:64, one launch (start us, length us, event | category | flops | bytes accessed | tf_op | source)
XLA Modules:
  0.0 181.6 jit_solution(4568837224232888138)
XLA Ops:
  1.3 177.4 %shard_map.180 = (f32[1024,512]{1,0:T(8,128)}, f32[16,2048]{1,0:T(8,128)}, f32[16,512]{1,0:T(8,128)}, f32[16,512]{1,0:T(8,128)}, f32[8,512]{1,0:T(8,128)}, /*index=5*/f32[8,128]{1,0:T(8,128)}, f32[8,384]{1,0:T(8,128)}) custom-call(bf16[1024,512]{1,0:T(8,128)(2,1)} %bitcast.7, s32[1,1024]{1,0:T(1,128)} %export_rows.1, s32[1,1024]{1,0:T(1,128)} %edge_src.1, ...), custom_call_target="tpu_custom_call" | custom-call | tf_op jit(solution)/shard_map/pallas_call | solution.py:553
  178.6 2.8 %shard_map.181 = (f32[1024,512]{1,0:T(8,128)}, f32[16,2048]{1,0:T(8,128)}, f32[16,512]{1,0:T(8,128)}, f32[16,512]{1,0:T(8,128)}, f32[8,512]{1,0:T(8,128)}, /*index=5*/f32[4,8]{1,0:T(4,128)}, f32[1,16]{1,0:T(1,128)}) custom-call(f32[1024,512]{1,0:T(8,128)} %get-tuple-element.21.refs_0_, f32[16,2048]{1,0:T(8,128)} %get-tuple-element.22.refs_1_, ...), custom_call_target="tpu_custom_call" | custom-call | tf_op jit(solution)/shard_map/pallas_call | solution.py:635

commit v9 on v8

--- a/solution.py
+++ b/solution.py
@@ -281,9 +281,12 @@
         cols = pl.ds(c * part, part)
 
         def to_slots(r):
-            slot_send[c, r, :] = dot(source_t[r, :], input_grad[:, cols]).astype(bf16)
-
-        blocks(slots, to_slots)
+            pair = dot(source_t[r, :], input_grad[:, c * part : (c + 2) * part]).astype(bf16)
+            slot_send[c, r, :] = pair[:, :part]
+            slot_send[c + 1, r, :] = pair[:, part:]
+
+        if c % 2 == 0:
+            blocks(slots, to_slots)
         pltpu.make_async_copy(
             slot_send.at[c, mine], slot_recv.at[c, mine], a_recv_sem.at[c]
         ).start()

time: 182 us -> 182 us (level)
  no operation moved by 1% of the time
where the time goes in v9:
time: 182 us
  Pallas kernels  180 us (99%)
    pallas_call x1, Pallas kernels, run_chain(): pl.pallas_call(chain_kernel, out_shape=(shape((rows, width), f32), shape(...  177 us

profile of v9, /device:TPU:64, one launch (start us, length us, event | category | flops | bytes accessed | tf_op | source)
XLA Modules:
  0.0 181.6 jit_solution(15665161720665130658)
XLA Ops:
  1.3 177.3 %shard_map.180 = (f32[1024,512]{1,0:T(8,128)}, f32[16,2048]{1,0:T(8,128)}, f32[16,512]{1,0:T(8,128)}, f32[16,512]{1,0:T(8,128)}, f32[8,512]{1,0:T(8,128)}, /*index=5*/f32[8,128]{1,0:T(8,128)}, f32[8,384]{1,0:T(8,128)}) custom-call(bf16[1024,512]{1,0:T(8,128)(2,1)} %bitcast.7, s32[1,1024]{1,0:T(1,128)} %export_rows.1, s32[1,1024]{1,0:T(1,128)} %edge_src.1, ...), custom_call_target="tpu_custom_call" | custom-call | tf_op jit(solution)/shard_map/pallas_call | solution.py:556
  178.6 2.8 %shard_map.181 = (f32[1024,512]{1,0:T(8,128)}, f32[16,2048]{1,0:T(8,128)}, f32[16,512]{1,0:T(8,128)}, f32[16,512]{1,0:T(8,128)}, f32[8,512]{1,0:T(8,128)}, /*index=5*/f32[4,8]{1,0:T(4,128)}, f32[1,16]{1,0:T(1,128)}) custom-call(f32[1024,512]{1,0:T(8,128)} %get-tuple-element.21.refs_0_, f32[16,2048]{1,0:T(8,128)} %get-tuple-element.22.refs_1_, ...), custom_call_target="tpu_custom_call" | custom-call | tf_op jit(solution)/shard_map/pallas_call | solution.py:638
